TPU v7x, 256 devices: a whole 4x4x8 slice. The times are simulated.
256 devices in a mesh: lat: 8 (over y, z_hi), lon: 32 (over x, z_lo, core).
Axes of the slice: x: 4, y: 4, z: 8 (z_hi: 2, z_lo: 4; z = z_hi * 4 + z_lo), core: 2. Of those that a mesh axis runs over, the one named last changes fastest.
Arguments:
- sea_level: float32 [4096, 1024], P('lon', 'lat'), may hold values from -1 to 5
- east_velocity: float32 [4096, 1024], P('lon', 'lat'), may hold values from -6 to 6
- north_velocity: float32 [4096, 1024], P('lon', 'lat'), may hold values from -6 to 6
- depth: float32 [4096, 1024], P('lon', 'lat'), may hold values from 0.25 to 1
- land_mask: int32 [4096, 1024], P('lon', 'lat'), may hold values from 0 to 1, as said below
- wet_counts: int32 [8, 32], replicated, may hold values from 1 to 16384, as said below
- loading_prev: float32 [4096, 1024], P('lon', 'lat'), may hold values from -4 to 4
- tide_amp: float32 [8], replicated, may hold values from 0.3 to 1
- tide_phase: float32 [8], replicated, may hold values from -3.140625 to 3.140625
- legendre: bfloat16 [1024, 1024, 1024], P('lon', None, 'lat'), may hold values from -0.1875 to 0.1875
- love_factor: float32 [1024], replicated, may hold values from 0.05 to 1
Outputs:
- height_new: float32 [4096, 1024], P('lon', 'lat')
- east_new: float32 [4096, 1024], P('lon', 'lat')
- north_new: float32 [4096, 1024], P('lon', 'lat')
- self_attraction: float32 [4096, 1024], P('lon', 'lat')
Inputs may be any that keep to these rules, and one draw needn't show every extreme that they name: `land_mask`: every tile of 128 columns by 128 rows holds at least one wet column, and one tile is wholly wet. wet_counts[p, q] is the number of wet columns of land_mask in latitude band p and longitude band q.
All inputs are finite; a program needn't handle non-finite values.
Results may differ from a plain program's by a relative error of at most 0.0038.
Values may be sent and summed in bfloat16 or wider, within the bound.
A program may use at most 64 MiB of HBM per device.

v0:
```python
import math

import jax
import jax.numpy as jnp
from jax import lax
from jax.sharding import Mesh
from jax.sharding import PartitionSpec as P

SUBSTEPS = 4
LON = ("lon_0", "lon_1", "lon_2")
LAT = ("lat_0", "lat_1")
LAT_LON = ("lat_0", "lat_1", "lon_0", "lon_1", "lon_2")


lat_edge = 1.3089969
courant = 0.4
friction = 0.02
rotation = 0.2
frequencies = (0.1405, 0.1454, 0.1379, 0.1458, 0.0729, 0.0676, 0.0725, 0.0649)
orders = (2, 2, 2, 2, 1, 1, 1, 1)
highest = lax.Precision.HIGHEST


def padded(cells, sides, width, closed):
    for axis, dim in sides:
        count = lax.axis_size(axis)
        ends = count if closed else count - 1
        head = lax.slice_in_dim(cells, 0, width, axis=dim)
        tail = lax.slice_in_dim(cells, cells.shape[dim] - width, cells.shape[dim], axis=dim)
        cells = jnp.concatenate(
            [
                lax.ppermute(tail, axis, [(i, (i + 1) % count) for i in range(ends)]),
                cells,
                lax.ppermute(head, axis, [((i + 1) % count, i) for i in range(ends)]),
            ],
            axis=dim,
        )
    return cells


def one_axis_at_a_time(value, axes):
    for axis in axes:
        value = lax.psum(value, axis)
    return value


def in_blocks(value, dim, size):
    before, after = (value.shape[:dim], value.shape[dim + 1 :])
    return jnp.moveaxis(value.reshape(*before, size, -1, *after), dim, 0)


def sum_at_owner(value, axis, dim):
    size = lax.axis_size(axis)
    tiles = lax.all_to_all(in_blocks(value, dim, size), axis, 0, 0, tiled=True)
    return jnp.sum(tiles, axis=0)


def from_everyone(value, axis):
    copies = jnp.broadcast_to(value, (lax.axis_size(axis), *value.shape))
    return lax.all_to_all(copies, axis, split_axis=0, concat_axis=0, tiled=True)


def of_everyone(value, axis):
    return from_everyone(value, axis).sum(axis=0)


def latitude_of(rows, total_rows):
    return -lat_edge + 2.0 * lat_edge * (rows.astype(jnp.float32) + 0.5) / total_rows


def potential(columns, rows, moment, total_cols, total_rows, tide_amp, tide_phase):
    longitude = (2.0 * math.pi * (columns % total_cols).astype(jnp.float32) / total_cols)[:, None]
    latitude = latitude_of(rows, total_rows)[None, :]
    semi = jnp.cos(latitude) ** 2
    diurnal = jnp.sin(2.0 * latitude)
    field = jnp.zeros((columns.shape[0], rows.shape[0]), jnp.float32)
    for index in range(len(frequencies)):
        shape_term = semi if orders[index] == 2 else diurnal
        field = field + tide_amp[index] * shape_term * jnp.cos(
            frequencies[index] * moment + orders[index] * longitude + tide_phase[index]
        )
    return field * (total_cols / 64.0)


def advance(state_x, static_x, forcing, latitude_x):
    height_x, east_x, north_x = (state_x[0], state_x[1], state_x[2])
    depth_x, wet_x, loading_x = (static_x[0], static_x[1], static_x[2])
    cosine = jnp.cos(latitude_x)[None, :]
    secant_cycle = (1.0 / jnp.cos(latitude_x[1:-1]))[None, :]
    secant_core = (1.0 / jnp.cos(latitude_x[2:-2]))[None, :]
    coriolis = (rotation * jnp.sin(latitude_x[2:-2]))[None, :]
    flux_east = depth_x * east_x
    flux_north = depth_x * north_x * cosine
    divergence = (
        (
            flux_east[2:, 1:-1]
            - flux_east[:-2, 1:-1]
            + (flux_north[1:-1, 2:] - flux_north[1:-1, :-2])
        )
        * 0.5
        * secant_cycle
    )
    height_cycle = height_x[1:-1, 1:-1] - courant * divergence * wet_x[1:-1, 1:-1]
    pressure = height_cycle - forcing - loading_x[1:-1, 1:-1]
    slope_east = (pressure[2:, 1:-1] - pressure[:-2, 1:-1]) * 0.5 * secant_core
    slope_north = (pressure[1:-1, 2:] - pressure[1:-1, :-2]) * 0.5
    east = east_x[2:-2, 2:-2]
    north = north_x[2:-2, 2:-2]
    wet = wet_x[2:-2, 2:-2]
    east_next = wet * ((1.0 - friction) * east + courant * (coriolis * north - slope_east))
    north_next = wet * ((1.0 - friction) * north - courant * (coriolis * east + slope_north))
    return jnp.stack([height_cycle[1:-1, 1:-1], east_next, north_next])


def extend_margin(fields, margin):
    wide = padded(fields, ((LON, 1),), margin, True)
    return padded(wide, ((LAT, 2),), margin, False)


def wave_table(waves, columns, total_cols, weights):
    turns = waves[None, :] * columns[:, None] % total_cols
    angle = 2.0 * math.pi * turns.astype(jnp.float32) / total_cols
    scale = weights[None, :] / math.sqrt(total_cols)
    return jnp.stack([scale * jnp.cos(angle), -scale * jnp.sin(angle)], axis=2)


def shards(
    sea_level,
    east_velocity,
    north_velocity,
    depth,
    land_mask,
    wet_counts,
    loading_prev,
    tide_amp,
    tide_phase,
    legendre,
    love_factor,
):
    lon_dev, lat_dev = sea_level.shape
    wave_dev = legendre.shape[0]
    lon_count = lax.axis_size(LON)
    total_cols = lon_dev * lon_count
    total_rows = lat_dev * lax.axis_size(LAT)
    lon_index = lax.axis_index(LON)
    lon_start = lon_index * lon_dev
    lat_start = lax.axis_index(LAT) * lat_dev
    wet = land_mask.astype(jnp.float32)
    margin = 2 * SUBSTEPS
    full = extend_margin(
        jnp.stack([sea_level, east_velocity, north_velocity, depth, wet, loading_prev]), margin
    )
    state_x = full[:3]
    static_full = full[3:]
    wide_cols = full.shape[1]
    wide_rows = full.shape[2]
    for moment in range(SUBSTEPS):
        reach = margin - 2 * moment
        offset = margin - reach
        static_x = static_full[:, offset : wide_cols - offset, offset : wide_rows - offset]
        latitude_x = jnp.clip(
            latitude_of(
                lat_start + jnp.arange(-reach, lat_dev + reach, dtype=jnp.int32), total_rows
            ),
            -1.5,
            1.5,
        )
        columns = lon_start + jnp.arange(1 - reach, lon_dev + reach - 1, dtype=jnp.int32)
        rows = lat_start + jnp.arange(1 - reach, lat_dev + reach - 1, dtype=jnp.int32)
        forcing = potential(
            columns, rows, float(moment), total_cols, total_rows, tide_amp, tide_phase
        )
        state_x = advance(state_x, static_x, forcing, latitude_x)
    height = state_x[0]
    wet_sum = one_axis_at_a_time(jnp.sum(wet * height), LAT_LON)
    mean_level = wet_sum / jnp.sum(wet_counts.astype(jnp.float32))
    anomaly = wet * (height - mean_level)
    local_cols = lon_start + jnp.arange(lon_dev, dtype=jnp.int32)
    count = wave_dev * lax.axis_size(LON)
    waves = jnp.arange(count, dtype=jnp.int32)
    table = wave_table(waves, local_cols, total_cols, jnp.ones((count,), jnp.float32))
    table = jnp.transpose(table, (1, 2, 0)).reshape(2 * count, lon_dev)
    fourier = sum_at_owner(
        jnp.dot(table, anomaly, precision=highest, preferred_element_type=jnp.float32).reshape(
            count, 2, lat_dev
        ),
        LON,
        0,
    ).astype(jnp.bfloat16)
    coefficients = lax.dot_general(
        fourier, legendre, (((2,), (2,)), ((0,), (0,))), preferred_element_type=jnp.float32
    )
    coefficients = of_everyone(coefficients, LAT)
    scaled = (coefficients * love_factor[None, None, :]).astype(jnp.bfloat16)
    synthesis = lax.dot_general(
        scaled, legendre, (((2,), (1,)), ((0,), (0,))), preferred_element_type=jnp.float32
    )
    own_waves = lon_index * wave_dev + jnp.arange(wave_dev, dtype=jnp.int32)
    weights = jnp.where(own_waves == 0, 1.0, 2.0).astype(jnp.float32)
    flat_spectra = synthesis.reshape(2 * wave_dev, lat_dev)
    count = lon_dev * lax.axis_size(LON)
    cells = jnp.arange(count, dtype=jnp.int32)
    table = wave_table(own_waves, cells, total_cols, weights).reshape(count, 2 * wave_dev)
    self_attraction = sum_at_owner(
        jnp.dot(table, flat_spectra, precision=highest, preferred_element_type=jnp.float32), LON, 0
    )
    return (state_x[0], state_x[1], state_x[2], self_attraction)


def solution(mesh):
    torus = Mesh(mesh.devices.reshape(4, 2, 4, 4, 2), ("lat_0", "lat_1", "lon_0", "lon_1", "lon_2"))
    return jax.shard_map(
        shards,
        mesh=torus,
        in_specs=(
            P(LON, LAT),
            P(LON, LAT),
            P(LON, LAT),
            P(LON, LAT),
            P(LON, LAT),
            P(),
            P(LON, LAT),
            P(),
            P(),
            P(LON, None, LAT),
            P(),
        ),
        out_specs=(P(LON, LAT), P(LON, LAT), P(LON, LAT), P(LON, LAT)),
        check_vma=False,
    )
```

profile of v0, /device:TPU:1, one launch (start us, length us, event | category | flops | bytes accessed | tf_op | source)
XLA Modules:
  0.0 320.3 jit_solution(9844729480353911763)
XLA Ops:
  5.7 3.3 %collective-permute-start.1 = (f32[6,8,128]{2,1,0:T(8,128)S(1)}, f32[6,8,128]{2,1,0:T(8,128)S(1)}, u32[]{:S(2)}, u32[]{:S(2)}) collective-permute-start(f32[6,8,128]{2,1,0:T(8,128)S(1)} %get-tuple-element.50), channel_id=1, source_target_pairs={{1,0},{2,1},{3,2},{4,3},{5,4},{6,5},{7,6},{8,7},{9,8},{10,9},{11,1... | collective-permute-start | bytes 73736 | tf_op jit(solution)/shard_map/ppermute | solution.py:34
  9.1 1.6 fusion.112
  13.2 1.6 fusion.111
  17.5 1.4 add_cosine_fusion.2
  22.7 1.4 add_cosine_fusion.4
  24.1 1.4 add_cosine_fusion.12
  36.0 1.4 add_cosine_fusion.18
  38.6 1.4 add_cosine_fusion.20
  49.3 1.4 add_cosine_fusion.28
  55.2 1.4 collective-permute-start.3
  56.6 8.8 %collective-permute-start.2 = (f32[6,144,8]{2,1,0:T(8,128)S(1)}, f32[6,144,8]{2,1,0:T(8,128)S(1)}, u32[]{:S(2)}, u32[]{:S(2)}) collective-permute-start(f32[6,144,8]{2,1,0:T(8,128)S(1)} %get-tuple-element.47), channel_id=1, source_target_pairs={{0,32},{32,64},{64,96},{96,128},{128,160},{160,192},{192,224},{1,3... | collective-permute-start | bytes 82952 | tf_op jit(solution)/shard_map/ppermute | solution.py:32
  65.4 4.6 %collective-permute-done.3 = f32[6,144,8]{2,1,0:T(8,128)S(1)} collective-permute-done((f32[6,144,8]{2,1,0:T(8,128)S(1)}, f32[6,144,8]{2,1,0:T(8,128)S(1)}, u32[]{:S(2)}, u32[]{:S(2)}) %collective-permute-start.3) | collective-permute-done | bytes 27680 | tf_op jit(solution)/shard_map/ppermute | solution.py:34
  70.0 1.4 collective-permute-done.2
  76.6 27.8 %psum.35 = f32[]{:T(128)} all-reduce(f32[]{:T(128)} %get-tuple-element.4), channel_id=1, replica_groups=mesh['lat_0'=4,'lat_1'=2,'lon_0'=4,'lon_1'=4,'lon_2'=2] {'lat_0'}, use_global_device_ids=true, to_apply=%region_1.2 | all-reduce | flops 1 | bytes 8 | tf_op jit(solution)/shard_map/psum | solution.py:43
  104.4 2.1 cosine_multiply_fusion
  106.6 8.6 %psum.36 = f32[]{:T(128)} all-reduce(f32[]{:T(128)} %psum.35), channel_id=1, replica_groups=mesh['lat_0'=4,'lat_1'=2,'lon_0'=4,'lon_1'=4,'lon_2'=2] {'lat_1'}, use_global_device_ids=true, to_apply=%region_2.3 | all-reduce | flops 1 | bytes 8 | tf_op jit(solution)/shard_map/psum | solution.py:43
  115.3 11.1 %psum.37 = f32[]{:T(128)} all-reduce(f32[]{:T(128)} %psum.36), channel_id=1, replica_groups=mesh['lat_0'=4,'lat_1'=2,'lon_0'=4,'lon_1'=4,'lon_2'=2] {'lon_0'}, use_global_device_ids=true, to_apply=%region_3.4 | all-reduce | flops 1 | bytes 8 | tf_op jit(solution)/shard_map/psum | solution.py:43
  127.0 18.4 %psum.38 = f32[]{:T(128)} all-reduce(f32[]{:T(128)} %psum.37), channel_id=1, replica_groups=mesh['lat_0'=4,'lat_1'=2,'lon_0'=4,'lon_1'=4,'lon_2'=2] {'lon_1'}, use_global_device_ids=true, to_apply=%region_4.5 | all-reduce | flops 1 | bytes 8 | tf_op jit(solution)/shard_map/psum | solution.py:43
  145.7 10.4 %psum.39 = f32[]{:T(128)} all-reduce(f32[]{:T(128)} %psum.38), channel_id=1, replica_groups=mesh['lat_0'=4,'lat_1'=2,'lon_0'=4,'lon_1'=4,'lon_2'=2] {'lon_2'}, use_global_device_ids=true, to_apply=%region_5.6 | all-reduce | flops 1 | bytes 8 | tf_op jit(solution)/shard_map/psum | solution.py:43
  158.4 31.0 %all_to_all.15 = f32[32,32,2,128]{3,1,2,0:T(8,128)S(1)} all-to-all(f32[32,32,2,128]{3,1,2,0:T(8,128)S(1)} %fusion.2), channel_id=1, replica_groups=mesh['lat_0'=4,'lat_1'=2,'lon_0'=4,'lon_1'=4,'lon_2'=2] {'lon_0','lon_1'..., dimensions={0} | all-to-all | bytes 2097152 | tf_op jit(solution)/shard_map/all_to_all | solution.py:54
  189.5 5.6 %fusion.83 = f32[32,2,1024]{2,1,0:T(2,128)S(1)} fusion(bf16[32,1024,128]{2,1,0:T(8,128)(2,1)} %param.20, bf16[32,2,128]{2,0,1:T(8,128)(2,1)S(1)} %reduce_sum.47), kind=kOutput, calls=%fused_computation.148 | convolution fusion | flops 16777216 | bytes 8667136 | tf_op jit(solution)/shard_map/dot_general | solution.py:190
  195.2 1.6 broadcast_in_dim.10
  196.8 7.1 %all-to-all-start.1 = ((f32[8,32,2,1024]{3,1,2,0:T(8,128)}), f32[8,32,2,1024]{3,1,2,0:T(8,128)S(1)}, u32[]{:S(2)}, u32[]{:S(2)}) async-start(f32[8,32,2,1024]{3,1,2,0:T(8,128)} %broadcast_in_dim.10), calls=%async_computation.1 | async-start | bytes 4194304 | tf_op jit(solution)/shard_map/all_to_all | solution.py:60
  204.0 2.1 cosine_multiply_fusion.1
  206.2 1.8 copy.30
  208.0 2.1 dot_general.16
  210.2 44.3 %all-to-all-done.1 = f32[8,32,2,1024]{3,1,2,0:T(8,128)S(1)} async-done(((f32[8,32,2,1024]{3,1,2,0:T(8,128)}), f32[8,32,2,1024]{3,1,2,0:T(8,128)S(1)}, u32[]{:S(2)}, u32[]{:S(2)}) %all-to-all-start.1) | async-done | bytes 2097184 | tf_op jit(solution)/shard_map/all_to_all | solution.py:60
  254.6 4.6 %fusion.64 = f32[32,2,128]{2,1,0:T(2,128)S(1)} fusion(bf16[32,1024,128]{2,1,0:T(8,128)(2,1)} %param.20, bf16[32,2,1024]{2,0,1:T(8,128)(2,1)S(1)} %multiply_convert_fusion), kind=kOutput, calls=%fused_computation.120 | convolution fusion | flops 16777216 | bytes 8552448 | tf_op jit(solution)/shard_map/dot_general | solution.py:195
  259.2 5.1 %fusion = f32[32,128,128]{2,1,0:T(8,128)} fusion(f32[64,128,1]{1,0,2:T(8,128)S(1)} %bitcast.95, f32[32,128,64]{1,0,2:T(8,128)S(1)} %dot_general.16), kind=kOutput, calls=%fused_computation.2 | convolution fusion | flops 402653184 | bytes 3178496 | tf_op jit(solution)/shard_map/dot_general | solution.py:205
  264.2 5.5 %all-to-all-start.2 = ((f32[32,128,128]{2,1,0:T(8,128)}), f32[32,128,128]{2,1,0:T(8,128)S(1)}, u32[]{:S(2)}, u32[]{:S(2)}) async-start(f32[32,128,128]{2,1,0:T(8,128)} %fusion), calls=%async_computation.2 | async-start | bytes 4194304 | tf_op jit(solution)/shard_map/all_to_all | solution.py:54
  269.9 1.9 fusion.72
  271.8 47.8 %all-to-all-done.2 = f32[32,128,128]{2,1,0:T(8,128)S(1)} async-done(((f32[32,128,128]{2,1,0:T(8,128)}), f32[32,128,128]{2,1,0:T(8,128)S(1)}, u32[]{:S(2)}, u32[]{:S(2)}) %all-to-all-start.2) | async-done | bytes 2097184 | tf_op jit(solution)/shard_map/all_to_all | solution.py:54
  (87 shorter events, 48.0 us)
Async XLA Ops:
  5.7 49.2 %collective-permute-start.1 = (f32[6,8,128]{2,1,0:T(8,128)S(1)}, f32[6,8,128]{2,1,0:T(8,128)S(1)}, u32[]{:S(2)}, u32[]{:S(2)}) collective-permute-start(f32[6,8,128]{2,1,0:T(8,128)S(1)} %get-tuple-element.50), channel_id=1, source_target_pairs={{1,0},{2,1},{3,2},{4,3},{5,4},{6,5},{7,6},{8,7},{9,8},{10,9},{11,1... | collective-permute-start | bytes 73736 | tf_op jit(solution)/shard_map/ppermute | solution.py:34
  9.0 45.9 %collective-permute-start = (f32[6,8,128]{2,1,0:T(8,128)S(1)}, f32[6,8,128]{2,1,0:T(8,128)S(1)}, u32[]{:S(2)}, u32[]{:S(2)}) collective-permute-start(f32[6,8,128]{2,1,0:T(8,128)S(1)} %get-tuple-element.49), channel_id=1, source_target_pairs={{0,1},{1,2},{2,3},{3,4},{4,5},{5,6},{6,7},{7,8},{8,9},{9,10},{10,1... | collective-permute-start | bytes 73736 | tf_op jit(solution)/shard_map/ppermute | solution.py:32
  55.2 20.7 %copy-start.1 = (s32[128,128]{1,0:T(8,128)S(1)}, s32[128,128]{1,0:T(8,128)}, u32[]{:S(2)}) copy-start(s32[128,128]{1,0:T(8,128)} %param.15) | copy-start | bytes 196612
  55.2 14.8 %collective-permute-start.3 = (f32[6,144,8]{2,1,0:T(8,128)S(1)}, f32[6,144,8]{2,1,0:T(8,128)S(1)}, u32[]{:S(2)}, u32[]{:S(2)}) collective-permute-start(f32[6,144,8]{2,1,0:T(8,128)S(1)} %get-tuple-element.48), channel_id=1, source_target_pairs={{32,0},{64,32},{96,64},{128,96},{160,128},{192,160},{224,192},{33,... | collective-permute-start | bytes 82952 | tf_op jit(solution)/shard_map/ppermute | solution.py:34
  56.6 14.8 %collective-permute-start.2 = (f32[6,144,8]{2,1,0:T(8,128)S(1)}, f32[6,144,8]{2,1,0:T(8,128)S(1)}, u32[]{:S(2)}, u32[]{:S(2)}) collective-permute-start(f32[6,144,8]{2,1,0:T(8,128)S(1)} %get-tuple-element.47), channel_id=1, source_target_pairs={{0,32},{32,64},{64,96},{96,128},{128,160},{160,192},{192,224},{1,3... | collective-permute-start | bytes 82952 | tf_op jit(solution)/shard_map/ppermute | solution.py:32
  71.9 4.0 %copy-start = (f32[132,132]{1,0:T(8,128)}, f32[132,132]{1,0:T(8,128)S(1)}, u32[]{:S(2)}) copy-start(f32[132,132]{1,0:T(8,128)S(1)} %get-tuple-element.43) | copy-start | bytes 209092
  72.1 54.3 %copy-start.4 = (s32[8,32]{1,0:T(8,128)S(1)}, s32[8,32]{1,0:T(8,128)}, u32[]{:S(2)}) copy-start(s32[8,32]{1,0:T(8,128)} %param.16) | copy-start | bytes 3076
  76.6 118.5 %copy-start.2 = (f32[128,128]{1,0:T(8,128)}, f32[128,128]{1,0:T(8,128)S(1)}, u32[]{:S(2)}) copy-start(f32[128,128]{1,0:T(8,128)S(1)} %get-tuple-element.5) | copy-start | bytes 196612
  195.1 59.4 %copy-start.3 = (f32[1024]{0:T(1024)S(1)}, f32[1024]{0:T(1024)}, u32[]{:S(2)}) copy-start(f32[1024]{0:T(1024)} %param.21) | copy-start | bytes 12292
  196.8 57.6 %all-to-all-start.1 = ((f32[8,32,2,1024]{3,1,2,0:T(8,128)}), f32[8,32,2,1024]{3,1,2,0:T(8,128)S(1)}, u32[]{:S(2)}, u32[]{:S(2)}) async-start(f32[8,32,2,1024]{3,1,2,0:T(8,128)} %broadcast_in_dim.10), calls=%async_computation.1 | async-start | bytes 4194304 | tf_op jit(solution)/shard_map/all_to_all | solution.py:60
  264.2 55.3 %all-to-all-start.2 = ((f32[32,128,128]{2,1,0:T(8,128)}), f32[32,128,128]{2,1,0:T(8,128)S(1)}, u32[]{:S(2)}, u32[]{:S(2)}) async-start(f32[32,128,128]{2,1,0:T(8,128)} %fusion), calls=%async_computation.2 | async-start | bytes 4194304 | tf_op jit(solution)/shard_map/all_to_all | solution.py:54
where the time goes:
time: 322 us; the launch traced here: 320 us
  blocking collectives  107 us (33%)
  waiting for transfers between devices  98 us (30%)
  other arithmetic  56.1 us (17%)
  starting transfers between devices  26.2 us (8%)
  matrix products  16.3 us (5%)
  local copies, waits for them, and re-layouts  14.1 us (4%)
    psum x5, blocking collectives, one_axis_at_a_time(): value = lax.psum(value, axis)  76.3 us
    all_to_all x1, waiting for transfers between devices, sum_at_owner(): tiles = lax.all_to_all(in_blocks(value, dim, size), axis, 0, 0, tiled=True)  47.8 us
    all_to_all x1, waiting for transfers between devices, from_everyone(): return lax.all_to_all(copies, axis, split_axis=0, concat_axis=0, tiled=True)  44.3 us
    all_to_all x1, blocking collectives, sum_at_owner(): tiles = lax.all_to_all(in_blocks(value, dim, size), axis, 0, 0, tiled=True)  31 us
    cos x16, other arithmetic, potential(): jnp.cos(frequencies[index] * moment + orders[index] * longitude + tide_ph...  21.2 us
    mul x16, other arithmetic, potential(): tide_amp[index] * shape_term  20.3 us
    ppermute x2, starting transfers between devices, padded(): lax.ppermute(tail, axis, [(i, (i + 1) % count) for i in range(ends)])  8.8 us
    all_to_all x1, starting transfers between devices, from_everyone(): return lax.all_to_all(copies, axis, split_axis=0, concat_axis=0, tiled=True)  7.15 us
  transfers between devices with their start and end apart: 6, of which 4 were waited for; matrix products, arithmetic and copies ran while one was open for 17% of the time, Pallas kernels for 0%

commit v1 on v0

v1 whole, which is shorter than its diff:
```python
import functools
import math

import jax
import jax.numpy as jnp
import ml_dtypes
import numpy as np
from jax import lax
from jax.experimental import pallas as pl
from jax.experimental.pallas import tpu as pltpu
from jax.sharding import PartitionSpec as P

SUBSTEPS = 4
NLON = 4096
NLAT = 1024
NDEG = 1024
LONS = 32
LATS = 8
TILE = 128
WAVES = 32
ROWS = TILE // LONS
MARGIN = 8
WIDE = TILE + 2 * MARGIN
FIELDS = 6

lat_edge = 1.3089969
courant = 0.4
friction = 0.02
rotation = 0.2
frequencies = (0.1405, 0.1454, 0.1379, 0.1458, 0.0729, 0.0676, 0.0725, 0.0649)
orders = (2, 2, 2, 2, 1, 1, 1, 1)
highest = lax.Precision.HIGHEST
MESH = pl.DeviceIdType.MESH
f32 = jnp.float32
bf16 = jnp.bfloat16


def turn(product, period):
    angle = 2.0 * np.pi * (product % period) / period
    return np.cos(angle), np.sin(angle)


def make_tables():
    band = np.arange(32)
    cell = np.arange(128)
    cos, sin = turn(np.outer(band, band), 32)
    first = np.zeros((8, 2, 32, 32, 8))
    for row in range(8):
        first[row, 0, :, :, row] = cos
        first[row, 1, :, :, row] = -sin
    first = first.reshape(512, 256)
    cos, sin = turn(np.outer(band, cell), 4096)
    twist = np.stack([cos, sin])
    cos, sin = turn(np.outer(band, cell), 128)
    second = np.zeros((32, 8, 2, 2, 128))
    for kind in range(2):
        second[:, 2 * kind, kind, 0] = cos / 64.0
        second[:, 2 * kind, kind, 1] = sin / 64.0
        second[:, 2 * kind + 1, kind, 0] = -sin / 64.0
        second[:, 2 * kind + 1, kind, 1] = cos / 64.0
    second = second.reshape(256, 512)
    place = np.zeros((32, 8, 4, 2, 128))
    spread = np.zeros((32, 2, 4, 2, 128))
    for s in range(32):
        for row in range(4):
            for r in range(2):
                place[s, r, row, r, 4 * s + row] = 1.0
                spread[s, r, row, r, 4 * s + row] = 1.0
    place = place.reshape(256, 1024)
    spread = spread.reshape(64, 1024)
    cos, sin = turn(np.outer(cell, band), 128)
    back = np.zeros((2, 128, 32, 2))
    back[0, :, :, 0] = cos
    back[0, :, :, 1] = -sin
    back[1, :, :, 0] = sin
    back[1, :, :, 1] = cos
    back = back.reshape(256, 64)
    cos, sin = turn(np.outer(cell, band), 4096)
    untwist = np.stack([np.tile(cos, (1, 4)), np.tile(sin, (1, 4))])
    cos, sin = turn(np.outer(band, band), 32)
    last = np.zeros((32, 4, 2, 4, 32))
    for row in range(4):
        last[:, row, 0, row, :] = cos
        last[:, row, 1, row, :] = -sin
    last = last.reshape(128, 256)
    wide = [first, twist, second, back, untwist, last]
    return [x.astype(np.float32) for x in wide] + [
        x.astype(ml_dtypes.bfloat16) for x in (place, spread)
    ]


def stencil(fields, la, north_table, tide):
    h, u, v, depth, wet, loading = fields
    cos, sec, coriolis, semi, diurnal = north_table

    def up(x, axis):
        return pltpu.roll(x, x.shape[axis] - 1, axis)

    def down(x, axis):
        return pltpu.roll(x, 1, axis)

    for moment in range(SUBSTEPS):
        forcing = semi * tide[moment][0] + diurnal * tide[moment][1]
        flux_east = depth * u
        flux_north = depth * v * cos
        divergence = (
            (up(flux_east, 0) - down(flux_east, 0) + (up(flux_north, 1) - down(flux_north, 1)))
            * 0.5
            * sec
        )
        h = h - courant * divergence * wet
        pressure = h - forcing - loading
        slope_east = (up(pressure, 0) - down(pressure, 0)) * 0.5 * sec
        slope_north = (up(pressure, 1) - down(pressure, 1)) * 0.5
        u, v = (
            wet * ((1.0 - friction) * u + courant * (coriolis * v - slope_east)),
            wet * ((1.0 - friction) * v - courant * (coriolis * u + slope_north)),
        )
    return h, u, v


def kernel(
    sea_ref, east_ref, north_ref, depth_ref, mask_ref, load_ref, tide_ref, counts_ref, love_ref,
    leg_hbm, first_hbm, twist_hbm, second_hbm, back_hbm, untwist_hbm, last_hbm, place_hbm, spread_hbm,
    h_out, u_out, v_out, s_out,
    leg, first, twist, second, back, untwist, last, place, spread,
    up_send, dn_send, lo_recv, hi_recv, lf_send, rt_send, lf_recv, rt_recv, dg_send, dg_recv, turned,
    sum_send, sum_recv, a1s, a1r, a2s, a2r, cs, cr, sg, a3s, a3r, a4s, a4r,
    local_sem, halo_send, halo_recv, many_send, many_recv,
):
    la = lax.axis_index("lat")
    lo = lax.axis_index("lon")

    def at(lat, lon):
        return {"lat": lat % LATS, "lon": lon % LONS}

    pairs = (
        (leg_hbm, leg), (first_hbm, first), (twist_hbm, twist), (second_hbm, second), (back_hbm, back),
        (untwist_hbm, untwist), (last_hbm, last), (place_hbm, place), (spread_hbm, spread),
    )
    loads = [
        pltpu.make_async_copy(src, dst, local_sem.at[i]) for i, (src, dst) in enumerate(pairs)
    ]

    barrier = pltpu.get_barrier_semaphore()

    def greet_lon(j, carry):
        pl.semaphore_signal(barrier, inc=1, device_id=at(la, lo + j), device_id_type=MESH)
        return carry

    def greet_lat(j, carry):
        pl.semaphore_signal(barrier, inc=1, device_id=at(la + j, lo), device_id_type=MESH)
        return carry

    lax.fori_loop(1, LATS, greet_lat, 0)
    for dl in (1, LATS - 1):
        for dn in (1, LONS - 1):
            pl.semaphore_signal(barrier, inc=1, device_id=at(la + dl, lo + dn), device_id_type=MESH)
    lax.fori_loop(1, LONS, greet_lon, 0)
    for load in loads:
        load.start()

    wet_core = mask_ref[...].astype(f32)
    cores = [sea_ref[...], east_ref[...], north_ref[...], depth_ref[...], wet_core, load_ref[...]]
    lane = lax.broadcasted_iota(jnp.int32, (TILE, TILE), 1)
    packed = jnp.zeros((TILE, TILE), f32)
    for f in range(FIELDS):
        moved = pltpu.roll(cores[f], 16 * f + 8, 1)
        packed = jnp.where((lane >= 16 * f) & (lane < 16 * f + 16), moved, packed)
        lf_send[f] = cores[f][0:8]
        rt_send[f] = cores[f][TILE - 8 : TILE]
    dg_send[0] = packed[0:8]
    dg_send[1] = packed[TILE - 8 : TILE]
    packed_t = packed.T
    for f in range(FIELDS):
        up_send[8 * f : 8 * f + 8] = packed_t[16 * f : 16 * f + 8]
        dn_send[8 * f : 8 * f + 8] = packed_t[16 * f + 8 : 16 * f + 16]

    pl.semaphore_wait(barrier, LONS - 1 + LATS - 1 + 4)

    moves = (
        (up_send, lo_recv, at(la + 1, lo)),
        (dn_send, hi_recv, at(la + LATS - 1, lo)),
        (lf_send, rt_recv, at(la, lo + LONS - 1)),
        (rt_send, lf_recv, at(la, lo + 1)),
        (dg_send.at[0], dg_recv.at[1, 0], at(la + 1, lo + LONS - 1)),
        (dg_send.at[0], dg_recv.at[1, 1], at(la + LATS - 1, lo + LONS - 1)),
        (dg_send.at[1], dg_recv.at[0, 0], at(la + 1, lo + 1)),
        (dg_send.at[1], dg_recv.at[0, 1], at(la + LATS - 1, lo + 1)),
    )
    halo = [
        pltpu.make_async_remote_copy(
            src_ref=src, dst_ref=dst, send_sem=halo_send.at[i], recv_sem=halo_recv.at[i],
            device_id=dev, device_id_type=MESH,
        )
        for i, (src, dst, dev) in enumerate(moves)
    ]
    for move in halo:
        move.start()

    slot = lax.broadcasted_iota(jnp.int32, (1, 2 * TILE), 1)
    row = la * TILE + jnp.where(slot < 192, slot, slot - 256)
    phi = -lat_edge + 2.0 * lat_edge * (row.astype(f32) + 0.5) / NLAT
    phi = jnp.clip(phi, -1.5, 1.5)
    cos = jnp.cos(phi)
    sec = 1.0 / cos
    coriolis = rotation * jnp.sin(phi)
    semi = cos * cos * (NLON / 64.0)
    diurnal = jnp.sin(2.0 * phi) * (NLON / 64.0)
    column = lo * TILE + lax.broadcasted_iota(jnp.int32, (WIDE, TILE), 0) + (NLON - MARGIN)
    lam = 2.0 * math.pi * (column % NLON).astype(f32) / NLON
    waves = tide_ref[0:1] * jnp.cos(tide_ref[2:3] * lam + tide_ref[1:2])
    wide_lane = lax.broadcasted_iota(jnp.int32, (WIDE, TILE), 1)
    tide = []
    for moment in range(SUBSTEPS):
        pair = []
        for kind in range(2):
            low = 8 * moment + 4 * kind
            inside = (wide_lane >= low) & (wide_lane < low + 4)
            pair.append(jnp.sum(jnp.where(inside, waves, 0.0), axis=1, keepdims=True))
        tide.append(pair)

    for move in halo:
        move.wait_recv()

    has_lo = jnp.where(la > 0, 1.0, 0.0).astype(f32)
    has_hi = jnp.where(la < LATS - 1, 1.0, 0.0).astype(f32)
    for f in range(FIELDS):
        turned[16 * f : 16 * f + 8] = lo_recv[8 * f : 8 * f + 8] * has_lo
        turned[16 * f + 8 : 16 * f + 16] = hi_recv[8 * f : 8 * f + 8] * has_hi
    turned[16 * FIELDS :] = jnp.zeros((TILE - 16 * FIELDS, TILE), f32)
    middle = turned[...].T
    short = lax.broadcasted_iota(jnp.int32, (8, TILE), 1) % 16 < 8
    ends = [
        jnp.where(short, dg_recv[side, 0] * has_lo, dg_recv[side, 1] * has_hi) for side in range(2)
    ]
    edges = jnp.concatenate([ends[0], middle, ends[1]], axis=0)
    fields = []
    for f in range(FIELDS):
        core = jnp.concatenate([lf_recv[f], cores[f], rt_recv[f]], axis=0)
        edge = pltpu.roll(edges, TILE - (16 * f + 8), 1)
        fields.append(jnp.concatenate([core, edge], axis=1))

    h, u, v = stencil(fields, la, (cos, sec, coriolis, semi, diurnal), tide)
    h = h[MARGIN : MARGIN + TILE, 0:TILE]
    h_out[...] = h
    u_out[...] = u[MARGIN : MARGIN + TILE, 0:TILE]
    v_out[...] = v[MARGIN : MARGIN + TILE, 0:TILE]
    wet_h = wet_core * h

    sum_send[...] = jnp.broadcast_to(jnp.sum(wet_h, keepdims=True), (8, TILE))
    sum_recv[pl.ds(la, 1)] = sum_send[...][None]

    def send_sum(j, carry):
        pltpu.make_async_remote_copy(
            src_ref=sum_send, dst_ref=sum_recv.at[la], send_sem=many_send.at[0],
            recv_sem=many_recv.at[0], device_id=at(la + j, lo), device_id_type=MESH,
        ).start()
        return carry

    lax.fori_loop(1, LATS, send_sum, 0)

    def exchange(index, source, target):
        def send(j, carry):
            peer = (lo + j) % LONS
            pltpu.make_async_remote_copy(
                src_ref=source.at[peer], dst_ref=target.at[lo], send_sem=many_send.at[index],
                recv_sem=many_recv.at[index], device_id=at(la, peer), device_id_type=MESH,
            ).start()
            return carry

        target[pl.ds(lo, 1)] = source[pl.ds(lo, 1)]
        lax.fori_loop(1, LONS, send, 0)

    def take(sems, index, buffer, count):
        part = buffer.at[pl.ds(0, count)]
        pltpu.make_async_copy(part, part, sems.at[index]).wait()

    wet_h_t = wet_h.T
    wet_t = wet_core.T
    for s in range(LONS):
        a1s[s, 0:ROWS] = wet_h_t[ROWS * s : ROWS * s + ROWS]
        a1s[s, ROWS : 2 * ROWS] = wet_t[ROWS * s : ROWS * s + ROWS]
    exchange(1, a1s, a1r)
    for load in loads[1:4]:
        load.wait()
    take(many_recv, 1, a1r, LONS - 1)
    spectra = jnp.dot(first[...], a1r[...].reshape(256, TILE), precision=highest, preferred_element_type=f32)
    cos_t = twist[0]
    sin_t = twist[1]
    blocks = []
    for l in range(ROWS):
        parts = []
        for kind in range(2):
            start = 64 * (4 * kind + l)
            re = spectra[start : start + 32]
            im = spectra[start + 32 : start + 64]
            parts += [re * cos_t + im * sin_t, im * cos_t - re * sin_t]
        blocks.append(jnp.concatenate(parts, axis=1))
    twisted = jnp.concatenate(blocks, axis=0)
    full = lax.dot_general(
        second[...], twisted, (((1,), (1,)), ((), ())), precision=highest, preferred_element_type=f32
    )
    take(many_recv, 0, sum_recv, LATS - 1)
    band_sum = jnp.sum(sum_recv[...], axis=0)[0:1]
    kind_row = lax.broadcasted_iota(jnp.int32, (256, TILE), 0) % 8
    full = jnp.where(kind_row == 4, band_sum, full)
    a2s[...] = full.reshape(LONS, 8, TILE)
    exchange(2, a2s, a2r)
    loads[7].wait()
    loads[0].wait()
    take(many_recv, 2, a2r, LONS - 1)
    got = a2r[...].reshape(256, TILE)
    total = jnp.sum(jnp.where(kind_row == 4, got, 0.0), axis=0, keepdims=True)
    mean = total / jnp.sum(counts_ref[...].astype(f32), keepdims=True)
    fourier = (got - mean * pltpu.roll(got, 254, 0)).astype(bf16)
    placed = lax.dot_general(
        fourier, place[...], (((0,), (0,)), ((), ())), preferred_element_type=f32
    )
    waves_r = []
    for r in range(2):
        value = placed[0:32, 128 * r : 128 * r + 128]
        for l in range(1, ROWS):
            start = 256 * l + 128 * r
            value = value + placed[32 * l : 32 * l + 32, start : start + 128]
        waves_r.append(value)

    sub = lax.broadcasted_iota(jnp.int32, (16, TILE), 0) % 8
    for g in range(4):
        pair = jnp.concatenate([waves_r[0][8 * g : 8 * g + 8], waves_r[1][8 * g : 8 * g + 8]], axis=0)
        acc = jnp.zeros((16, NDEG), f32)
        for t in range(4):
            lhs = jnp.concatenate(
                [jnp.where(sub == 2 * t, pair, 0.0), jnp.where(sub == 2 * t + 1, pair, 0.0)], axis=1
            ).astype(bf16)
            rhs = jnp.concatenate([leg[8 * g + 2 * t], leg[8 * g + 2 * t + 1]], axis=1)
            acc = acc + lax.dot_general(
                lhs, rhs, (((1,), (1,)), ((), ())), preferred_element_type=f32
            )
        for d in range(LATS):
            cs[d, 16 * g : 16 * g + 16] = acc[:, 128 * d : 128 * d + 128]

    cr[pl.ds(la, 1)] = cs[pl.ds(la, 1)]

    def send_coefficients(j, carry):
        peer = (la + j) % LATS
        pltpu.make_async_remote_copy(
            src_ref=cs.at[peer], dst_ref=cr.at[la], send_sem=many_send.at[3],
            recv_sem=many_recv.at[3], device_id=at(peer, lo), device_id_type=MESH,
        ).start()
        return carry

    lax.fori_loop(1, LATS, send_coefficients, 0)
    love = love_ref[pl.ds(la, 1)]
    take(many_recv, 3, cr, LATS - 1)
    coefficients = jnp.sum(cr[...], axis=0)
    sg[pl.ds(la, 1)] = (coefficients * love).astype(bf16)[None]

    def send_scaled(j, carry):
        pltpu.make_async_remote_copy(
            src_ref=sg.at[la], dst_ref=sg.at[la], send_sem=many_send.at[4],
            recv_sem=many_recv.at[4], device_id=at(la + j, lo), device_id_type=MESH,
        ).start()
        return carry

    lax.fori_loop(1, LATS, send_scaled, 0)
    for load in loads[4:7] + loads[8:9]:
        load.wait()
    take(many_recv, 4, sg, LATS - 1)

    heads = []
    for g in range(4):
        lhs = jnp.concatenate([sg[d, 16 * g : 16 * g + 16] for d in range(LATS)], axis=1)
        acc = jnp.zeros((16, TILE), f32)
        for t in range(4):
            rhs = jnp.concatenate([leg[8 * g + 2 * t], leg[8 * g + 2 * t + 1]], axis=1)
            both = jnp.dot(lhs, rhs, preferred_element_type=f32)
            acc = jnp.where(sub == 2 * t, both[:, 0:TILE], acc)
            acc = jnp.where(sub == 2 * t + 1, both[:, TILE:], acc)
        if g == 0:
            weight = jnp.where((sub == 0) & (lo == 0), 1.0 / 64.0, 2.0 / 64.0)
            acc = acc * weight
        else:
            acc = acc * (2.0 / 64.0)
        heads.append(acc)
    both = jnp.concatenate(
        [
            jnp.concatenate([heads[g][0:8] for g in range(4)], axis=0),
            jnp.concatenate([heads[g][8:16] for g in range(4)], axis=0),
        ],
        axis=1,
    )
    empty = jnp.zeros((WAVES, 256), f32)
    stacked = jnp.concatenate(
        [
            jnp.concatenate([both if c == l else empty for c in range(ROWS)], axis=1)
            for l in range(ROWS)
        ],
        axis=0,
    )
    large = stacked.astype(bf16)
    small = (stacked - large.astype(f32)).astype(bf16)
    rows = lax.dot_general(
        spread[...], large, (((1,), (1,)), ((), ())), preferred_element_type=f32
    ) + lax.dot_general(spread[...], small, (((1,), (1,)), ((), ())), preferred_element_type=f32)
    for s in range(LONS):
        a3s[s] = rows[2 * s : 2 * s + 2]
    exchange(5, a3s, a3r)
    take(many_recv, 5, a3r, LONS - 1)
    waves_all = jnp.concatenate([a3r[s] for s in range(LONS)], axis=0)
    opened = jnp.dot(back[...], waves_all, precision=highest, preferred_element_type=f32)
    re = opened[0:TILE]
    im = opened[TILE:]
    cos_u = untwist[0]
    sin_u = untwist[1]
    untwisted = jnp.concatenate([re * cos_u - im * sin_u, re * sin_u + im * cos_u], axis=1)
    field = lax.dot_general(
        last[...], untwisted, (((1,), (1,)), ((), ())), precision=highest, preferred_element_type=f32
    )
    for s in range(LONS):
        a4s[s] = field[ROWS * s : ROWS * s + ROWS]
    exchange(6, a4s, a4r)
    take(many_recv, 6, a4r, LONS - 1)
    s_out[...] = jnp.concatenate([a4r[s] for s in range(LONS)], axis=0).T

    for move in halo:
        move.wait_send()
    take(many_send, 0, sum_recv, LATS - 1)
    take(many_send, 1, a1s, LONS - 1)
    take(many_send, 2, a2s, LONS - 1)
    take(many_send, 3, cs, LATS - 1)
    take(many_send, 4, sg, LATS - 1)
    take(many_send, 5, a3s, LONS - 1)
    take(many_send, 6, a4s, LONS - 1)


def shards(
    sea_level, east_velocity, north_velocity, depth, land_mask, wet_counts, loading_prev,
    tide_amp, tide_phase, legendre, love_factor,
):
    moments = jnp.arange(SUBSTEPS, dtype=f32)[:, None]
    phase = (moments * jnp.array(frequencies, f32)[None, :] + tide_phase[None, :]).reshape(32)
    amp = jnp.tile(tide_amp, SUBSTEPS)
    order = jnp.tile(jnp.array(orders, f32), SUBSTEPS)
    tide = jnp.pad(jnp.stack([amp, phase, order]), ((0, 5), (0, TILE - 32)))
    tables = make_tables()
    vmem = pl.BlockSpec(memory_space=pltpu.VMEM)
    hbm = pl.BlockSpec(memory_space=pl.ANY)
    shape = jax.ShapeDtypeStruct((TILE, TILE), f32)
    scratch = [pltpu.VMEM((WAVES, NDEG, TILE), bf16)]
    scratch += [pltpu.VMEM(x.shape, x.dtype) for x in tables]
    scratch += [
        pltpu.VMEM((48, TILE), f32), pltpu.VMEM((48, TILE), f32),
        pltpu.VMEM((48, TILE), f32), pltpu.VMEM((48, TILE), f32),
        pltpu.VMEM((FIELDS, 8, TILE), f32), pltpu.VMEM((FIELDS, 8, TILE), f32),
        pltpu.VMEM((FIELDS, 8, TILE), f32), pltpu.VMEM((FIELDS, 8, TILE), f32),
        pltpu.VMEM((2, 8, TILE), f32), pltpu.VMEM((2, 2, 8, TILE), f32),
        pltpu.VMEM((TILE, TILE), f32),
        pltpu.VMEM((8, TILE), f32), pltpu.VMEM((LATS, 8, TILE), f32),
        pltpu.VMEM((LONS, 8, TILE), f32), pltpu.VMEM((LONS, 8, TILE), f32),
        pltpu.VMEM((LONS, 8, TILE), f32), pltpu.VMEM((LONS, 8, TILE), f32),
        pltpu.VMEM((LATS, 64, TILE), f32), pltpu.VMEM((LATS, 64, TILE), f32),
        pltpu.VMEM((LATS, 64, TILE), bf16),
        pltpu.VMEM((LONS, 2, TILE), f32), pltpu.VMEM((LONS, 2, TILE), f32),
        pltpu.VMEM((LONS, ROWS, TILE), f32), pltpu.VMEM((LONS, ROWS, TILE), f32),
        pltpu.SemaphoreType.DMA((9,)),
        pltpu.SemaphoreType.DMA((8,)), pltpu.SemaphoreType.DMA((8,)),
        pltpu.SemaphoreType.DMA((7,)), pltpu.SemaphoreType.DMA((7,)),
    ]
    return pl.pallas_call(
        kernel,
        out_shape=(shape,) * 4,
        in_specs=[vmem] * 9 + [hbm] * 9,
        out_specs=(vmem,) * 4,
        scratch_shapes=scratch,
        compiler_params=pltpu.CompilerParams(
            collective_id=0, has_side_effects=True, vmem_limit_bytes=40 * 1024 * 1024
        ),
        name="tide",
    )(
        sea_level, east_velocity, north_velocity, depth, land_mask, loading_prev, tide, wet_counts,
        love_factor.reshape(LATS, NDEG // LATS), legendre, *[jnp.asarray(x) for x in tables],
    )


def solution(mesh):
    grid = P("lon", "lat")
    return jax.shard_map(
        shards,
        mesh=mesh,
        in_specs=(grid, grid, grid, grid, grid, P(), grid, P(), P(), P("lon", None, "lat"), P()),
        out_specs=(grid, grid, grid, grid),
        check_vma=False,
    )
```

time: 322 us -> 89.7 us (0.28)
  blocking collectives: 107 us -> 0 us
  waiting for transfers between devices: 98 us -> 0 us
  Pallas kernels: 0 us -> 66.2 us
  other arithmetic: 56.1 us -> 0.7 us
  starting transfers between devices: 26.2 us -> 0 us
  matrix products: 16.3 us -> 0 us
  local copies, waits for them, and re-layouts: 14.1 us -> 21.4 us
    all_to_all x2 -> x0, waiting for transfers between devices: 92 us -> none  [the longest x1 47.8 us: sum_at_owner(): tiles = lax.all_to_all(in_blocks(value, dim, size), axis, 0, 0, tiled=True)]
    psum x5 -> x0, blocking collectives: 76.3 us -> none  [one_axis_at_a_time(): value = lax.psum(value, axis)]
    pallas_call x0 -> x1, Pallas kernels: none -> 66.2 us  [shards(): pl.pallas_call(kernel, out_shape=(shape,) * 4, in_specs=[vmem] * 9 + [hbm...]
    all_to_all x1 -> x0, blocking collectives: 31 us -> none  [sum_at_owner(): tiles = lax.all_to_all(in_blocks(value, dim, size), axis, 0, 0, tiled=True)]
    mul x31 -> x0, other arithmetic: 29.1 us -> none  [the longest x16 20.3 us: potential(): tide_amp[index] * shape_term]
    cos x16 -> x0, other arithmetic: 21.2 us -> none  [potential(): jnp.cos(frequencies[index] * moment + orders[index] * longitude + tide_ph...]
    unnamed x14 -> x38, local copies, waits for them, and re-layouts: 3.4 us -> 19.8 us
    dot_general x4 -> x0, matrix products: 16.3 us -> none  [the longest x1 5.64 us: shards(): lax.dot_general(fourier, legendre, (((2,), (2,)), ((0,), (0,))), preferre...]
  transfers between devices with their start and end apart: 6 -> 0, of which waited for: 4 -> 0; matrix products, arithmetic and copies ran while one was open for 17% -> 0% of each run, Pallas kernels for 0% -> 0%
where the time goes in v1:
time: 89.7 us; the launch traced here: 89 us
  Pallas kernels  66.2 us (74%)
  local copies, waits for them, and re-layouts  21.4 us (24%)
    pallas_call x1, Pallas kernels, shards(): pl.pallas_call(kernel, out_shape=(shape,) * 4, in_specs=[vmem] * 9 + [hbm...  66.2 us
    unnamed x38, local copies, waits for them, and re-layouts  19.8 us

profile of v1, /device:TPU:1, one launch (start us, length us, event | category | flops | bytes accessed | tf_op | source)
XLA Modules:
  0.0 89.0 jit_solution(13690791675800746772)
XLA Ops:
  0.6 0.7 multiply_add_fusion
  1.3 0.1 add.22
  1.4 0.7 tile.5
  2.1 0.1 stack_tile.7
  2.1 0.7 tile.4
  2.8 0.1 stack_tile.6
  2.9 0.0 copy-start
  2.9 3.4 %copy-done = bf16[32,1024,128]{2,1,0:T(8,128)(2,1)S(1)} copy-done((bf16[32,1024,128]{2,1,0:T(8,128)(2,1)S(1)}, bf16[32,1024,128]{2,1,0:T(8,128)(2,1)}, u32[]{:S(2)}) %copy-start) | copy-done | bytes 8388632
  6.3 0.0 copy-start.1
  6.3 1.0 %copy-done.1 = bf16[256,1024]{1,0:T(8,128)(2,1)S(1)} copy-done((bf16[256,1024]{1,0:T(8,128)(2,1)S(1)}, bf16[256,1024]{1,0:T(8,128)(2,1)}, u32[]{:S(2)}) %copy-start.1) | copy-done | bytes 524312
  7.3 0.0 copy-start.2
  7.3 1.0 %copy-done.2 = f32[256,512]{1,0:T(8,128)S(1)} copy-done((f32[256,512]{1,0:T(8,128)S(1)}, f32[256,512]{1,0:T(8,128)}, u32[]{:S(2)}) %copy-start.2) | copy-done | bytes 524312
  8.4 0.0 copy-start.3
  8.4 1.0 %copy-done.3 = f32[512,256]{1,0:T(8,128)S(1)} copy-done((f32[512,256]{1,0:T(8,128)S(1)}, f32[512,256]{1,0:T(8,128)}, u32[]{:S(2)}) %copy-start.3) | copy-done | bytes 524312
  9.4 0.9 %copy-done.4 = bf16[64,1024]{1,0:T(8,128)(2,1)S(1)} copy-done((bf16[64,1024]{1,0:T(8,128)(2,1)S(1)}, bf16[64,1024]{1,0:T(8,128)(2,1)}, u32[]{:S(2)}) %copy-start.4) | copy-done | bytes 131096
  10.3 0.9 %copy-done.5 = f32[128,256]{1,0:T(8,128)S(1)} copy-done((f32[128,256]{1,0:T(8,128)S(1)}, f32[128,256]{1,0:T(8,128)}, u32[]{:S(2)}) %copy-start.5) | copy-done | bytes 131096
  11.2 0.9 %copy-done.6 = f32[2,128,128]{2,1,0:T(8,128)S(1)} copy-done((f32[2,128,128]{2,1,0:T(8,128)S(1)}, f32[2,128,128]{2,1,0:T(8,128)}, u32[]{:S(2)}) %copy-start.6) | copy-done | bytes 131096
  12.1 0.9 %copy-done.7 = f32[256,64]{1,0:T(8,128)S(1)} copy-done((f32[256,64]{1,0:T(8,128)S(1)}, f32[256,64]{1,0:T(8,128)}, u32[]{:S(2)}) %copy-start.7) | copy-done | bytes 65560
  13.0 0.8 copy-done.8
  13.9 0.8 copy-done.9
  14.7 0.8 copy-done.10
  15.6 0.8 copy-done.11
  16.4 0.8 copy-done.12
  17.2 0.8 copy-done.13
  18.1 0.8 copy-done.14
  18.8 0.7 copy-done.15
  19.5 0.7 copy-done.16
  20.2 66.2 %tide.1 = (f32[128,128]{1,0:T(8,128)S(1)}, f32[128,128]{1,0:T(8,128)S(1)}, f32[128,128]{1,0:T(8,128)S(1)}, f32[128,128]{1,0:T(8,128)S(1)}) custom-call(f32[128,128]{1,0:T(8,128)S(1)} %copy-done.8, f32[128,128]{1,0:T(8,128)S(1)} %copy-done.9, f32[128,128]{1,0:T(8,128)S(1)} %copy-done.10, f32[128,128]{1,0:T(8,128)S(1)} %copy-done.11, ...), custom_call_target="tpu_custom_call" | custom-call | tf_op jit(solution)/shard_map/tide/pallas_call | solution.py:470
  86.5 0.6 copy.29
  87.1 0.6 copy.30
  87.7 0.6 copy.31
  88.3 0.6 copy.32
  (14 shorter events, 0.0 us)
Async XLA Ops:
  2.9 3.4 %copy-start = (bf16[32,1024,128]{2,1,0:T(8,128)(2,1)S(1)}, bf16[32,1024,128]{2,1,0:T(8,128)(2,1)}, u32[]{:S(2)}) copy-start(bf16[32,1024,128]{2,1,0:T(8,128)(2,1)} %leg_hbm.1) | copy-start | bytes 25165828
  6.3 1.0 %copy-start.1 = (bf16[256,1024]{1,0:T(8,128)(2,1)S(1)}, bf16[256,1024]{1,0:T(8,128)(2,1)}, u32[]{:S(2)}) copy-start(bf16[256,1024]{1,0:T(8,128)(2,1)} %constant.31.clone.place_hbm) | copy-start | bytes 1572868
  7.3 1.0 %copy-start.2 = (f32[256,512]{1,0:T(8,128)S(1)}, f32[256,512]{1,0:T(8,128)}, u32[]{:S(2)}) copy-start(f32[256,512]{1,0:T(8,128)} %constant.27.clone.second_hbm) | copy-start | bytes 1572868
  8.4 1.0 %copy-start.3 = (f32[512,256]{1,0:T(8,128)S(1)}, f32[512,256]{1,0:T(8,128)}, u32[]{:S(2)}) copy-start(f32[512,256]{1,0:T(8,128)} %constant.25.clone.first_hbm) | copy-start | bytes 1572868
  9.4 0.9 %copy-start.4 = (bf16[64,1024]{1,0:T(8,128)(2,1)S(1)}, bf16[64,1024]{1,0:T(8,128)(2,1)}, u32[]{:S(2)}) copy-start(bf16[64,1024]{1,0:T(8,128)(2,1)} %constant.32.clone.spread_hbm) | copy-start | bytes 393220
  10.3 0.9 %copy-start.5 = (f32[128,256]{1,0:T(8,128)S(1)}, f32[128,256]{1,0:T(8,128)}, u32[]{:S(2)}) copy-start(f32[128,256]{1,0:T(8,128)} %constant.30.clone.last_hbm) | copy-start | bytes 393220
  11.2 0.9 %copy-start.6 = (f32[2,128,128]{2,1,0:T(8,128)S(1)}, f32[2,128,128]{2,1,0:T(8,128)}, u32[]{:S(2)}) copy-start(f32[2,128,128]{2,1,0:T(8,128)} %constant.29.clone.untwist_hbm) | copy-start | bytes 393220
  12.1 0.9 %copy-start.7 = (f32[256,64]{1,0:T(8,128)S(1)}, f32[256,64]{1,0:T(8,128)}, u32[]{:S(2)}) copy-start(f32[256,64]{1,0:T(8,128)} %constant.28.clone.back_hbm) | copy-start | bytes 196612
  13.0 0.8 copy-start.8
  13.9 0.8 copy-start.9
  14.7 0.8 copy-start.10
  15.6 0.8 copy-start.11
  16.4 0.8 copy-start.12
  17.2 0.8 copy-start.13
  18.1 0.8 copy-start.14
  18.8 0.7 copy-start.15
  19.5 0.7 copy-start.16

commit v2 on v1

v2 whole, which is shorter than its diff:
```python
import functools
import math

import jax
import jax.numpy as jnp
import ml_dtypes
import numpy as np
from jax import lax
from jax.experimental import pallas as pl
from jax.experimental.pallas import tpu as pltpu
from jax.sharding import PartitionSpec as P

SUBSTEPS = 4
NLON = 4096
NLAT = 1024
NDEG = 1024
LONS = 32
LATS = 8
TILE = 128
WAVES = 32
ROWS = TILE // LONS
MARGIN = 8
WIDE = TILE + 2 * MARGIN
FIELDS = 6
SLOTS = 4
VMEM_BYTES = 56 * 1024 * 1024

lat_edge = 1.3089969
courant = 0.4
friction = 0.02
rotation = 0.2
frequencies = (0.1405, 0.1454, 0.1379, 0.1458, 0.0729, 0.0676, 0.0725, 0.0649)
orders = (2, 2, 2, 2, 1, 1, 1, 1)
highest = lax.Precision.HIGHEST
MESH = pl.DeviceIdType.MESH
f32 = jnp.float32
bf16 = jnp.bfloat16


def turn(product, period):
    angle = 2.0 * np.pi * (product % period) / period
    return np.cos(angle), np.sin(angle)


def split(table):
    high = table.astype(ml_dtypes.bfloat16)
    low = (table - high.astype(np.float64)).astype(ml_dtypes.bfloat16)
    return np.concatenate([high, high, low], axis=1)


def make_tables():
    band = np.arange(32)
    cell = np.arange(128)
    cos, sin = turn(np.outer(band, band), 32)
    first = np.zeros((ROWS, 2, 32, 32, ROWS))
    for row in range(ROWS):
        first[row, 0, :, :, row] = cos
        first[row, 1, :, :, row] = -sin
    first = first.reshape(256, 128)
    cos, sin = turn(np.outer(band, cell), 4096)
    extra = np.zeros((8, 128))
    extra[0, :32] = (np.arange(SUBSTEPS)[:, None] * np.array(frequencies)[None, :]).reshape(-1)
    extra[1, :32] = np.tile(np.array(orders), SUBSTEPS)
    twist = np.concatenate([cos, sin, extra])
    cos, sin = turn(np.outer(band, cell), 128)
    second = np.zeros((32, SLOTS, 2, 128))
    second[:, 0, 0] = cos / 64.0
    second[:, 0, 1] = sin / 64.0
    second[:, 1, 0] = -sin / 64.0
    second[:, 1, 1] = cos / 64.0
    second = second.reshape(128, 256)
    place = np.zeros((32, SLOTS, ROWS, 2, 128))
    for s in range(32):
        for row in range(ROWS):
            for r in range(2):
                place[s, r, row, r, ROWS * s + row] = 1.0
    spread = place[:, :2].reshape(64, 1024)
    place = place.reshape(128, 1024)
    cos, sin = turn(np.outer(cell, band), 128)
    back = np.zeros((2, 128, 32, 2))
    back[0, :, :, 0] = cos
    back[0, :, :, 1] = -sin
    back[1, :, :, 0] = sin
    back[1, :, :, 1] = cos
    back = back.reshape(256, 64)
    cos, sin = turn(np.outer(cell, band), 4096)
    untwist = np.stack([np.tile(cos, (1, ROWS)), np.tile(sin, (1, ROWS))])
    cos, sin = turn(np.outer(band, band), 32)
    last = np.zeros((32, ROWS, 2, ROWS, 32))
    for row in range(ROWS):
        last[:, row, 0, row, :] = cos
        last[:, row, 1, row, :] = -sin
    last = last.reshape(128, 256)
    plain = [x.astype(np.float32) for x in (twist, untwist)]
    exact = [x.astype(ml_dtypes.bfloat16) for x in (place, spread)]
    return [split(first), plain[0], split(second), exact[0], split(back), plain[1], split(last), exact[1]]


def halves(value, axis):
    high = value.astype(bf16)
    low = (value - high.astype(f32)).astype(bf16)
    return jnp.concatenate([high, low, high], axis=axis)


def stencil(fields, la, north_table, tide):
    h, u, v, depth, wet, loading = fields
    cos, sec, coriolis, semi, diurnal = north_table

    def up(x, axis):
        return pltpu.roll(x, x.shape[axis] - 1, axis)

    def down(x, axis):
        return pltpu.roll(x, 1, axis)

    for moment in range(SUBSTEPS):
        forcing = semi * tide[moment][0] + diurnal * tide[moment][1]
        flux_east = depth * u
        flux_north = depth * v * cos
        divergence = (
            (up(flux_east, 0) - down(flux_east, 0) + (up(flux_north, 1) - down(flux_north, 1)))
            * 0.5
            * sec
        )
        h = h - courant * divergence * wet
        pressure = h - forcing - loading
        slope_east = (up(pressure, 0) - down(pressure, 0)) * 0.5 * sec
        slope_north = (up(pressure, 1) - down(pressure, 1)) * 0.5
        u, v = (
            wet * ((1.0 - friction) * u + courant * (coriolis * v - slope_east)),
            wet * ((1.0 - friction) * v - courant * (coriolis * u + slope_north)),
        )
    return h, u, v


def across(lhs, rhs):
    return lax.dot_general(lhs, rhs, (((1,), (1,)), ((), ())), preferred_element_type=f32)


def kernel(
    sea_hbm, east_hbm, north_hbm, depth_hbm, mask_hbm, load_hbm, amp_hbm, phase_hbm, counts_hbm, love_hbm,
    leg_hbm, first_hbm, twist_hbm, second_hbm, place_hbm, back_hbm, untwist_hbm, last_hbm, spread_hbm,
    h_hbm, u_hbm, v_hbm, s_hbm,
    sea_ref, east_ref, north_ref, depth_ref, mask_ref, load_ref, amp_ref, phase_ref, counts_ref, love_ref,
    leg, first, twist, second, place, back, untwist, last, spread,
    up_send, dn_send, lo_recv, hi_recv, lf_send, rt_send, lf_recv, rt_recv, dg_send, dg_recv, turned,
    sum_send, sum_recv, a0s, a0r, a1s, a1r, aws, awr, a2s, a2r, lhs_ref, cs, cr, sg, acc_ref, a3s, a3r, a4s, a4r,
    h_out, u_out, v_out, s_out,
    local_sem, halo_send, halo_recv, many_send, many_recv, scaled_recv, store_sem,
):
    la = lax.axis_index("lat")
    lo = lax.axis_index("lon")

    def at(lat, lon):
        return {"lat": lat % LATS, "lon": lon % LONS}

    pairs = (
        (sea_hbm, sea_ref), (east_hbm, east_ref), (north_hbm, north_ref), (depth_hbm, depth_ref),
        (mask_hbm, mask_ref), (load_hbm, load_ref), (amp_hbm, amp_ref), (phase_hbm, phase_ref),
        (twist_hbm, twist), (first_hbm, first), (second_hbm, second), (place_hbm, place),
        (counts_hbm, counts_ref), (leg_hbm, leg), (love_hbm, love_ref), (spread_hbm, spread),
        (back_hbm, back), (untwist_hbm, untwist), (last_hbm, last),
    )
    loads = [
        pltpu.make_async_copy(src, dst, local_sem.at[i]) for i, (src, dst) in enumerate(pairs)
    ]
    for load in loads[0:6]:
        load.start()

    barrier = pltpu.get_barrier_semaphore()

    def greet_lon(j, carry):
        pl.semaphore_signal(barrier, inc=1, device_id=at(la, lo + j), device_id_type=MESH)
        return carry

    def greet_lat(j, carry):
        pl.semaphore_signal(barrier, inc=1, device_id=at(la + j, lo), device_id_type=MESH)
        return carry

    lax.fori_loop(1, LATS, greet_lat, 0)
    for dl in (1, LATS - 1):
        for dn in (1, LONS - 1):
            pl.semaphore_signal(barrier, inc=1, device_id=at(la + dl, lo + dn), device_id_type=MESH)
    lax.fori_loop(1, LONS, greet_lon, 0)
    for load in loads[6:]:
        load.start()
    for load in loads[0:6]:
        load.wait()

    wet_core = mask_ref[...].astype(f32)
    cores = [sea_ref[...], east_ref[...], north_ref[...], depth_ref[...], wet_core, load_ref[...]]
    lane = lax.broadcasted_iota(jnp.int32, (TILE, TILE), 1)
    packed = jnp.zeros((TILE, TILE), f32)
    for f in range(FIELDS):
        moved = pltpu.roll(cores[f], 16 * f + 8, 1)
        packed = jnp.where((lane >= 16 * f) & (lane < 16 * f + 16), moved, packed)
        lf_send[f] = cores[f][0:8]
        rt_send[f] = cores[f][TILE - 8 : TILE]
    dg_send[0] = packed[0:8]
    dg_send[1] = packed[TILE - 8 : TILE]
    packed_t = packed.T
    for f in range(FIELDS):
        up_send[8 * f : 8 * f + 8] = packed_t[16 * f : 16 * f + 8]
        dn_send[8 * f : 8 * f + 8] = packed_t[16 * f + 8 : 16 * f + 16]
    wet_t = wet_core.T
    for s in range(LONS):
        a0s[s] = wet_t[ROWS * s : ROWS * s + ROWS]

    slot = lax.broadcasted_iota(jnp.int32, (1, 2 * TILE), 1)
    row = la * TILE + jnp.where(slot < 192, slot, slot - 256)
    phi = -lat_edge + 2.0 * lat_edge * (row.astype(f32) + 0.5) / NLAT
    phi = jnp.clip(phi, -1.5, 1.5)
    cos = jnp.cos(phi)
    sec = 1.0 / cos
    coriolis = rotation * jnp.sin(phi)
    semi = cos * cos * (NLON / 64.0)
    diurnal = jnp.sin(2.0 * phi) * (NLON / 64.0)
    for load in loads[6:9]:
        load.wait()
    short_lane = lax.broadcasted_iota(jnp.int32, (1, TILE), 1)
    amp = jnp.zeros((1, TILE), f32)
    phase = jnp.zeros((1, TILE), f32)
    for c in range(8):
        hit = (short_lane % 8 == c) & (short_lane < 8 * SUBSTEPS)
        amp = jnp.where(hit, amp_ref[c], amp)
        phase = jnp.where(hit, phase_ref[c], phase)
    phase = phase + twist[64:65]
    column = lo * TILE + lax.broadcasted_iota(jnp.int32, (WIDE, TILE), 0) + (NLON - MARGIN)
    lam = 2.0 * math.pi * (column % NLON).astype(f32) / NLON
    waves = amp * jnp.cos(twist[65:66] * lam + phase)
    wide_lane = lax.broadcasted_iota(jnp.int32, (WIDE, TILE), 1)
    tide = []
    for moment in range(SUBSTEPS):
        pair = []
        for kind in range(2):
            low = 8 * moment + 4 * kind
            inside = (wide_lane >= low) & (wide_lane < low + 4)
            pair.append(jnp.sum(jnp.where(inside, waves, 0.0), axis=1, keepdims=True))
        tide.append(pair)

    pl.semaphore_wait(barrier, LONS - 1 + LATS - 1 + 4)

    moves = (
        (up_send, lo_recv, at(la + 1, lo)),
        (dn_send, hi_recv, at(la + LATS - 1, lo)),
        (dg_send.at[0], dg_recv.at[1, 0], at(la + 1, lo + LONS - 1)),
        (dg_send.at[0], dg_recv.at[1, 1], at(la + LATS - 1, lo + LONS - 1)),
        (dg_send.at[1], dg_recv.at[0, 0], at(la + 1, lo + 1)),
        (dg_send.at[1], dg_recv.at[0, 1], at(la + LATS - 1, lo + 1)),
        (lf_send, rt_recv, at(la, lo + LONS - 1)),
        (rt_send, lf_recv, at(la, lo + 1)),
    )
    halo = [
        pltpu.make_async_remote_copy(
            src_ref=src, dst_ref=dst, send_sem=halo_send.at[i], recv_sem=halo_recv.at[i],
            device_id=dev, device_id_type=MESH,
        )
        for i, (src, dst, dev) in enumerate(moves)
    ]
    for move in halo:
        move.start()

    def exchange(index, source, target):
        def one(peer):
            pltpu.make_async_remote_copy(
                src_ref=source.at[peer], dst_ref=target.at[lo], send_sem=many_send.at[index],
                recv_sem=many_recv.at[index], device_id=at(la, peer), device_id_type=MESH,
            ).start()

        for dx in (2, 1, 3, 0):

            def send(j, carry, dx=dx):
                one((lo // 8 + dx) % 4 * 8 + (lo + j) % 8)
                return carry

            lax.fori_loop(1 if dx == 0 else 0, 8, send, 0)
        target[pl.ds(lo, 1)] = source[pl.ds(lo, 1)]

    def take(sems, index, buffer, count):
        part = buffer.at[pl.ds(0, count)]
        pltpu.make_async_copy(part, part, sems.at[index]).wait()

    def rows_of(buffer):
        return jnp.concatenate([buffer[s] for s in range(LONS)], axis=0)

    exchange(7, a0s, a0r)

    for move in halo:
        move.wait_recv()

    has_lo = jnp.where(la > 0, 1.0, 0.0).astype(f32)
    has_hi = jnp.where(la < LATS - 1, 1.0, 0.0).astype(f32)
    for f in range(FIELDS):
        turned[16 * f : 16 * f + 8] = lo_recv[8 * f : 8 * f + 8] * has_lo
        turned[16 * f + 8 : 16 * f + 16] = hi_recv[8 * f : 8 * f + 8] * has_hi
    turned[16 * FIELDS :] = jnp.zeros((TILE - 16 * FIELDS, TILE), f32)
    middle = turned[...].T
    short = lax.broadcasted_iota(jnp.int32, (8, TILE), 1) % 16 < 8
    ends = [
        jnp.where(short, dg_recv[side, 0] * has_lo, dg_recv[side, 1] * has_hi) for side in range(2)
    ]
    edges = jnp.concatenate([ends[0], middle, ends[1]], axis=0)
    fields = []
    for f in range(FIELDS):
        core = jnp.concatenate([lf_recv[f], cores[f], rt_recv[f]], axis=0)
        edge = pltpu.roll(edges, TILE - (16 * f + 8), 1)
        fields.append(jnp.concatenate([core, edge], axis=1))

    h, u, v = stencil(fields, la, (cos, sec, coriolis, semi, diurnal), tide)
    h = h[MARGIN : MARGIN + TILE, 0:TILE]
    wet_h = wet_core * h
    wet_h_t = wet_h.T
    for s in range(LONS):
        a1s[s] = wet_h_t[ROWS * s : ROWS * s + ROWS]
    sum_send[...] = jnp.broadcast_to(jnp.sum(wet_h, keepdims=True), (1, TILE))
    sum_recv[pl.ds(la, 1)] = sum_send[...][None]

    def send_sum(j, carry):
        pltpu.make_async_remote_copy(
            src_ref=sum_send, dst_ref=sum_recv.at[la], send_sem=many_send.at[0],
            recv_sem=many_recv.at[0], device_id=at(la + j, lo), device_id_type=MESH,
        ).start()
        return carry

    lax.fori_loop(1, LATS, send_sum, 0)
    exchange(1, a1s, a1r)
    h_out[...] = h
    u_out[...] = u[MARGIN : MARGIN + TILE, 0:TILE]
    v_out[...] = v[MARGIN : MARGIN + TILE, 0:TILE]
    stores = [
        pltpu.make_async_copy(src, dst, store_sem.at[i])
        for i, (src, dst) in enumerate(
            ((h_out, h_hbm), (u_out, u_hbm), (v_out, v_hbm), (s_out, s_hbm))
        )
    ]
    for store in stores[0:3]:
        store.start()

    def analyse(spectra):
        cos_t = twist[0:32]
        sin_t = twist[32:64]
        blocks = []
        for l in range(ROWS):
            re = spectra[64 * l : 64 * l + 32]
            im = spectra[64 * l + 32 : 64 * l + 64]
            blocks.append(
                jnp.concatenate([re * cos_t + im * sin_t, im * cos_t - re * sin_t], axis=1)
            )
        return across(second[...], halves(jnp.concatenate(blocks, axis=0), 1))

    for load in loads[9:12]:
        load.wait()
    take(many_recv, 7, a0r, LONS - 1)
    mask_rows = rows_of(a0r).astype(bf16)
    full = analyse(
        jnp.dot(
            first[:, TILE:], jnp.concatenate([mask_rows, mask_rows], axis=0), preferred_element_type=f32
        )
    )
    for s in range(LONS):
        aws[s] = full[SLOTS * s : SLOTS * s + SLOTS]
    exchange(8, aws, awr)
    take(many_recv, 0, sum_recv, LATS - 1)
    band_sum = jnp.sum(sum_recv[...], axis=0)
    take(many_recv, 1, a1r, LONS - 1)
    full = analyse(jnp.dot(first[...], halves(rows_of(a1r), 0), preferred_element_type=f32))
    kind_row = lax.broadcasted_iota(jnp.int32, (TILE, TILE), 0) % SLOTS
    full = jnp.where(kind_row == 2, band_sum, full)
    for s in range(LONS):
        a2s[s] = full[SLOTS * s : SLOTS * s + SLOTS]
    exchange(2, a2s, a2r)
    for load in loads[12:15]:
        load.wait()
    count = jnp.sum(counts_ref[...].astype(f32), keepdims=True)
    take(many_recv, 8, awr, LONS - 1)
    got_mask = rows_of(awr)
    take(many_recv, 2, a2r, LONS - 1)
    got = rows_of(a2r)
    total = jnp.sum(jnp.where(kind_row == 2, got, 0.0), axis=0, keepdims=True)
    fourier = (got - (total / count) * got_mask).astype(bf16)
    placed = lax.dot_general(
        fourier, place[...], (((0,), (0,)), ((), ())), preferred_element_type=f32
    )
    waves_r = []
    for r in range(2):
        value = placed[0:32, 128 * r : 128 * r + 128]
        for l in range(1, ROWS):
            start = 256 * l + 128 * r
            value = value + placed[32 * l : 32 * l + 32, start : start + 128]
        waves_r.append(value)

    sub = lax.broadcasted_iota(jnp.int32, (16, TILE), 0) % 8
    for g in range(4):
        pair = jnp.concatenate([waves_r[0][8 * g : 8 * g + 8], waves_r[1][8 * g : 8 * g + 8]], axis=0)
        for j in range(8):
            lhs_ref[g, :, TILE * j : TILE * j + TILE] = jnp.where(sub == j, pair, 0.0).astype(bf16)

    def send_coefficients(peer):
        pltpu.make_async_remote_copy(
            src_ref=cs.at[peer], dst_ref=cr.at[la], send_sem=many_send.at[3],
            recv_sem=many_recv.at[3], device_id=at(peer, lo), device_id_type=MESH,
        ).start()

    def analysis(t, carry):
        y = (la // 2 + 2 + t) % 4
        start = pl.multiple_of(y * 256, 256)
        for g in range(4):
            rhs = jnp.concatenate([leg[8 * g + j, pl.ds(start, 256), :] for j in range(8)], axis=1)
            acc = across(lhs_ref[g], rhs)
            cs[2 * y, 16 * g : 16 * g + 16] = acc[:, 0:TILE]
            cs[2 * y + 1, 16 * g : 16 * g + 16] = acc[:, TILE:]
        send_coefficients(2 * y + 1 - la % 2)

        @pl.when(t != 2)
        def _():
            send_coefficients(2 * y + la % 2)

        return carry

    lax.fori_loop(0, 4, analysis, 0)
    cr[pl.ds(la, 1)] = cs[pl.ds(la, 1)]
    love = love_ref[pl.ds(la, 1)]
    take(many_recv, 3, cr, LATS - 1)
    coefficients = jnp.sum(cr[...], axis=0)
    sg[pl.ds(la, 1)] = (coefficients * love).astype(bf16)[None]

    def send_scaled(j, carry):
        peer = (la + LATS - j) % LATS
        pltpu.make_async_remote_copy(
            src_ref=sg.at[la], dst_ref=sg.at[la], send_sem=many_send.at[4],
            recv_sem=scaled_recv.at[la], device_id=at(peer, lo), device_id_type=MESH,
        ).start()
        return carry

    lax.fori_loop(1, LATS, send_scaled, 0)
    for load in loads[15:]:
        load.wait()

    def take_scaled(owner):
        part = sg.at[owner]
        pltpu.make_async_copy(part, part, scaled_recv.at[owner]).wait()

    def synthesis(t, carry):
        y = (la // 2 + t) % 4

        @pl.when(t != 0)
        def _():
            take_scaled(2 * y + la % 2)

        take_scaled(2 * y + 1 - la % 2)
        start = pl.multiple_of(y * 256, 256)
        left = sg[2 * y]
        right = sg[2 * y + 1]
        for g in range(4):
            lhs = jnp.concatenate([left[16 * g : 16 * g + 16], right[16 * g : 16 * g + 16]], axis=1)
            for k in range(4):
                rhs = jnp.concatenate(
                    [leg[8 * g + 2 * k + i, pl.ds(start, 256), :] for i in range(2)], axis=1
                )
                acc_ref[4 * g + k] += jnp.dot(lhs, rhs, preferred_element_type=f32)
        return carry

    acc_ref[...] = jnp.zeros((16, 16, 256), f32)
    lax.fori_loop(0, 4, synthesis, 0)
    heads = []
    for g in range(4):
        acc = jnp.zeros((16, TILE), f32)
        for k in range(4):
            acc = jnp.where(sub == 2 * k, acc_ref[4 * g + k, :, 0:TILE], acc)
            acc = jnp.where(sub == 2 * k + 1, acc_ref[4 * g + k, :, TILE:], acc)
        if g == 0:
            weight = jnp.where((sub == 0) & (lo == 0), 1.0 / 64.0, 2.0 / 64.0)
            acc = acc * weight
        else:
            acc = acc * (2.0 / 64.0)
        heads.append(acc)
    both = jnp.concatenate(
        [
            jnp.concatenate([heads[g][0:8] for g in range(4)], axis=0),
            jnp.concatenate([heads[g][8:16] for g in range(4)], axis=0),
        ],
        axis=1,
    )
    empty = jnp.zeros((WAVES, 256), f32)
    stacked = jnp.concatenate(
        [
            jnp.concatenate([both if c == l else empty for c in range(ROWS)], axis=1)
            for l in range(ROWS)
        ],
        axis=0,
    )
    large = stacked.astype(bf16)
    tiny = (stacked - large.astype(f32)).astype(bf16)
    rows = across(spread[...], large) + across(spread[...], tiny)
    for s in range(LONS):
        a3s[s] = rows[2 * s : 2 * s + 2]
    exchange(5, a3s, a3r)
    take(many_recv, 5, a3r, LONS - 1)

    opened = jnp.dot(back[...], halves(rows_of(a3r), 0), preferred_element_type=f32)
    re = opened[0:TILE]
    im = opened[TILE:]
    cos_u = untwist[0]
    sin_u = untwist[1]
    untwisted = jnp.concatenate([re * cos_u - im * sin_u, re * sin_u + im * cos_u], axis=1)
    field = across(last[...], halves(untwisted, 1))
    for s in range(LONS):
        a4s[s] = field[ROWS * s : ROWS * s + ROWS]
    exchange(6, a4s, a4r)
    take(many_recv, 6, a4r, LONS - 1)
    s_out[...] = rows_of(a4r).T
    stores[3].start()

    for move in halo:
        move.wait_send()
    take(many_send, 0, sum_recv, LATS - 1)
    take(many_send, 1, a1s, LONS - 1)
    take(many_send, 2, a2s, LONS - 1)
    take(many_send, 3, cs, LATS - 1)
    take(many_send, 4, sg, LATS - 1)
    take(many_send, 5, a3s, LONS - 1)
    take(many_send, 6, a4s, LONS - 1)
    take(many_send, 7, a0s, LONS - 1)
    take(many_send, 8, aws, LONS - 1)
    for store in stores:
        store.wait()


def deliver(*refs):
    for i in range(4):
        refs[i + 4][...] = refs[i][...]


def shards(
    sea_level, east_velocity, north_velocity, depth, land_mask, wet_counts, loading_prev,
    tide_amp, tide_phase, legendre, love_factor,
):
    tables = make_tables()
    hbm = pl.BlockSpec(memory_space=pltpu.HBM)
    vmem = pl.BlockSpec(memory_space=pltpu.VMEM)
    shape = jax.ShapeDtypeStruct((TILE, TILE), f32)
    tile = pltpu.VMEM((TILE, TILE), f32)
    slab = pltpu.VMEM((FIELDS, 8, TILE), f32)
    edge = pltpu.VMEM((48, TILE), f32)
    quad = pltpu.VMEM((LONS, SLOTS, TILE), f32)
    two = pltpu.VMEM((LONS, 2, TILE), f32)
    part = pltpu.VMEM((LATS, 64, TILE), f32)
    scratch = [tile, tile, tile, tile, pltpu.VMEM((TILE, TILE), jnp.int32), tile]
    scratch += [pltpu.SMEM((8,), f32), pltpu.SMEM((8,), f32)]
    scratch += [pltpu.VMEM((LATS, LONS), jnp.int32), pltpu.VMEM((LATS, TILE), f32)]
    scratch += [pltpu.VMEM((WAVES, NDEG, TILE), bf16)]
    scratch += [pltpu.VMEM(x.shape, x.dtype) for x in tables]
    scratch += [edge, edge, edge, edge, slab, slab, slab, slab]
    scratch += [pltpu.VMEM((2, 8, TILE), f32), pltpu.VMEM((2, 2, 8, TILE), f32), tile]
    scratch += [pltpu.VMEM((1, TILE), f32), pltpu.VMEM((LATS, 1, TILE), f32)]
    scratch += [quad] * 8
    scratch += [pltpu.VMEM((4, 16, 8 * TILE), bf16), part, part, pltpu.VMEM((LATS, 64, TILE), bf16)]
    scratch += [pltpu.VMEM((16, 16, 2 * TILE), f32), two, two, quad, quad]
    scratch += [tile] * 4
    scratch += [
        pltpu.SemaphoreType.DMA((19,)),
        pltpu.SemaphoreType.DMA((8,)), pltpu.SemaphoreType.DMA((8,)),
        pltpu.SemaphoreType.DMA((9,)), pltpu.SemaphoreType.DMA((9,)), pltpu.SemaphoreType.DMA((8,)),
        pltpu.SemaphoreType.DMA((4,)),
    ]
    results = pl.pallas_call(
        kernel,
        out_shape=(shape,) * 4,
        in_specs=[hbm] * 19,
        out_specs=(hbm,) * 4,
        scratch_shapes=scratch,
        compiler_params=pltpu.CompilerParams(
            collective_id=0, has_side_effects=True, vmem_limit_bytes=VMEM_BYTES
        ),
        name="tide",
    )(
        sea_level, east_velocity, north_velocity, depth, land_mask, loading_prev, tide_amp, tide_phase,
        wet_counts, love_factor.reshape(LATS, NDEG // LATS), legendre,
        *[jnp.asarray(x) for x in tables],
    )
    return pl.pallas_call(
        deliver,
        out_shape=(shape,) * 4,
        in_specs=[vmem] * 4,
        out_specs=(vmem,) * 4,
        name="deliver",
    )(*results)


def solution(mesh):
    grid = P("lon", "lat")
    return jax.shard_map(
        shards,
        mesh=mesh,
        in_specs=(grid, grid, grid, grid, grid, P(), grid, P(), P(), P("lon", None, "lat"), P()),
        out_specs=(grid, grid, grid, grid),
        check_vma=False,
    )
```

time: 89.7 us -> 64.5 us (0.72)
  local copies, waits for them, and re-layouts: 21.4 us -> 0 us
  Pallas kernels: 66.2 us -> 63.7 us
    unnamed x38 -> x0, local copies, waits for them, and re-layouts: 19.8 us -> none
    pallas_call x1 -> x2, Pallas kernels: 66.2 us -> 63.7 us  [the longest x1 62 us: shards(): pl.pallas_call(kernel, out_shape=(shape,) * 4, in_specs=[hbm] * 19, out_s...]
    another operation x4 -> x0, local copies, waits for them, and re-layouts: 1.48 us -> none  [the longest x1 0.66 us: shards(): order = jnp.tile(jnp.array(orders, f32), SUBSTEPS)]
where the time goes in v2:
time: 64.5 us; the launch traced here: 64.3 us
  Pallas kernels  63.7 us (99%)
    pallas_call x1, Pallas kernels, shards(): pl.pallas_call(kernel, out_shape=(shape,) * 4, in_specs=[hbm] * 19, out_s...  62 us
    pallas_call x1, Pallas kernels, shards(): pl.pallas_call(deliver, out_shape=(shape,) * 4, in_specs=[vmem] * 4, out_...  1.64 us

profile of v2, /device:TPU:1, one launch (start us, length us, event | category | flops | bytes accessed | tf_op | source)
XLA Modules:
  0.0 64.3 jit_solution(9459880432021804480)
XLA Ops:
  0.6 62.0 %tide.1 = (f32[128,128]{1,0:T(8,128)}, f32[128,128]{1,0:T(8,128)}, f32[128,128]{1,0:T(8,128)}, f32[128,128]{1,0:T(8,128)}) custom-call(f32[128,128]{1,0:T(8,128)} %sea_hbm.1, f32[128,128]{1,0:T(8,128)} %east_hbm.1, f32[128,128]{1,0:T(8,128)} %north_hbm.1, f32[128,128]{1,0:T(8,128)} %depth_hbm.1, s32[128,128]{1,0:T(8,128)} %mask_hbm.1, f32[128,128]{1,0:T(8,128)} %load_hbm.1, ...), custom_call_target="tpu_custom_call" | custom-call | tf_op jit(solution)/shard_map/tide/pallas_call | solution.py:565
  62.7 1.6 %deliver.1 = (f32[128,128]{1,0:T(8,128)}, f32[128,128]{1,0:T(8,128)}, f32[128,128]{1,0:T(8,128)}, f32[128,128]{1,0:T(8,128)}) custom-call(f32[128,128]{1,0:T(8,128)} %get-tuple-element.8.refs_0_, f32[128,128]{1,0:T(8,128)} %get-tuple-element.9.refs_1_, f32[128,128]{1,0:T(8,128)} %get-tuple-element.10.refs_2_, f32[128,128]{1,0:T(8,128)} %get-tuple-element.11.refs_3_), custom_call_target="tpu_custom_call" | custom-call | tf_op jit(solution)/shard_map/deliver/pallas_call | solution.py:580

commit v3 on v2

--- a/solution.py
+++ b/solution.py
@@ -23,7 +23,8 @@
 WIDE = TILE + 2 * MARGIN
 FIELDS = 6
 SLOTS = 4
-VMEM_BYTES = 56 * 1024 * 1024
+QUARTER = NDEG // 4
+VMEM_BYTES = 40 * 1024 * 1024
 
 lat_edge = 1.3089969
 courant = 0.4
@@ -139,13 +140,12 @@
 def kernel(
     sea_hbm, east_hbm, north_hbm, depth_hbm, mask_hbm, load_hbm, amp_hbm, phase_hbm, counts_hbm, love_hbm,
     leg_hbm, first_hbm, twist_hbm, second_hbm, place_hbm, back_hbm, untwist_hbm, last_hbm, spread_hbm,
-    h_hbm, u_hbm, v_hbm, s_hbm,
+    h_out, u_out, v_out, s_out,
     sea_ref, east_ref, north_ref, depth_ref, mask_ref, load_ref, amp_ref, phase_ref, counts_ref, love_ref,
     leg, first, twist, second, place, back, untwist, last, spread,
     up_send, dn_send, lo_recv, hi_recv, lf_send, rt_send, lf_recv, rt_recv, dg_send, dg_recv, turned,
-    sum_send, sum_recv, a0s, a0r, a1s, a1r, aws, awr, a2s, a2r, lhs_ref, cs, cr, sg, acc_ref, a3s, a3r, a4s, a4r,
-    h_out, u_out, v_out, s_out,
-    local_sem, halo_send, halo_recv, many_send, many_recv, scaled_recv, store_sem,
+    sum_send, sum_recv, a0s, a0r, a1s, a1r, aws, awr, a2s, a2r, lhs_ref, cs, cr, cb, db, sg, acc_ref, a3s, a3r, a4s, a4r,
+    local_sem, halo_send, halo_recv, many_send, many_recv, scaled_recv,
 ):
     la = lax.axis_index("lat")
     lo = lax.axis_index("lon")
@@ -240,12 +240,12 @@
     pl.semaphore_wait(barrier, LONS - 1 + LATS - 1 + 4)
 
     moves = (
-        (up_send, lo_recv, at(la + 1, lo)),
-        (dn_send, hi_recv, at(la + LATS - 1, lo)),
         (dg_send.at[0], dg_recv.at[1, 0], at(la + 1, lo + LONS - 1)),
         (dg_send.at[0], dg_recv.at[1, 1], at(la + LATS - 1, lo + LONS - 1)),
         (dg_send.at[1], dg_recv.at[0, 0], at(la + 1, lo + 1)),
         (dg_send.at[1], dg_recv.at[0, 1], at(la + LATS - 1, lo + 1)),
+        (up_send, lo_recv, at(la + 1, lo)),
+        (dn_send, hi_recv, at(la + LATS - 1, lo)),
         (lf_send, rt_recv, at(la, lo + LONS - 1)),
         (rt_send, lf_recv, at(la, lo + 1)),
     )
@@ -308,10 +308,8 @@
     h, u, v = stencil(fields, la, (cos, sec, coriolis, semi, diurnal), tide)
     h = h[MARGIN : MARGIN + TILE, 0:TILE]
     wet_h = wet_core * h
-    wet_h_t = wet_h.T
-    for s in range(LONS):
-        a1s[s] = wet_h_t[ROWS * s : ROWS * s + ROWS]
-    sum_send[...] = jnp.broadcast_to(jnp.sum(wet_h, keepdims=True), (1, TILE))
+
+    sum_send[...] = jnp.sum(wet_h, axis=0, keepdims=True)
     sum_recv[pl.ds(la, 1)] = sum_send[...][None]
 
     def send_sum(j, carry):
@@ -322,18 +320,13 @@
         return carry
 
     lax.fori_loop(1, LATS, send_sum, 0)
+    wet_h_t = wet_h.T
+    for s in range(LONS):
+        a1s[s] = wet_h_t[ROWS * s : ROWS * s + ROWS]
     exchange(1, a1s, a1r)
     h_out[...] = h
     u_out[...] = u[MARGIN : MARGIN + TILE, 0:TILE]
     v_out[...] = v[MARGIN : MARGIN + TILE, 0:TILE]
-    stores = [
-        pltpu.make_async_copy(src, dst, store_sem.at[i])
-        for i, (src, dst) in enumerate(
-            ((h_out, h_hbm), (u_out, u_hbm), (v_out, v_hbm), (s_out, s_hbm))
-        )
-    ]
-    for store in stores[0:3]:
-        store.start()
 
     def analyse(spectra):
         cos_t = twist[0:32]
@@ -375,7 +368,7 @@
     got_mask = rows_of(awr)
     take(many_recv, 2, a2r, LONS - 1)
     got = rows_of(a2r)
-    total = jnp.sum(jnp.where(kind_row == 2, got, 0.0), axis=0, keepdims=True)
+    total = jnp.sum(jnp.where(kind_row == 2, got, 0.0), keepdims=True)
     fourier = (got - (total / count) * got_mask).astype(bf16)
     placed = lax.dot_general(
         fourier, place[...], (((0,), (0,)), ((), ())), preferred_element_type=f32
@@ -394,44 +387,51 @@
         for j in range(8):
             lhs_ref[g, :, TILE * j : TILE * j + TILE] = jnp.where(sub == j, pair, 0.0).astype(bf16)
 
-    def send_coefficients(peer):
+    near = la % 2
+    y_own = la // 2
+
+    def y_at(t):
+        return (y_own + 2 + t - t // 2 * (2 * t - 1)) % 4
+
+    def analysis(t, carry):
+        y = y_at(t)
+        start = pl.multiple_of(y * QUARTER, QUARTER)
+        for g in range(4):
+            rhs = jnp.concatenate([leg[8 * g + j, pl.ds(start, QUARTER), :] for j in range(8)], axis=1)
+            acc = across(lhs_ref[g], rhs)
+            cs[y, 16 * g : 16 * g + 16] = acc
+            cb[y, 16 * g : 16 * g + 16] = acc.astype(bf16)
         pltpu.make_async_remote_copy(
-            src_ref=cs.at[peer], dst_ref=cr.at[la], send_sem=many_send.at[3],
-            recv_sem=many_recv.at[3], device_id=at(peer, lo), device_id_type=MESH,
+            src_ref=cb.at[y], dst_ref=db.at[y_own], send_sem=many_send.at[9],
+            recv_sem=many_recv.at[9], device_id=at(2 * y + 1 - near, lo), device_id_type=MESH,
         ).start()
 
-    def analysis(t, carry):
-        y = (la // 2 + 2 + t) % 4
-        start = pl.multiple_of(y * 256, 256)
-        for g in range(4):
-            rhs = jnp.concatenate([leg[8 * g + j, pl.ds(start, 256), :] for j in range(8)], axis=1)
-            acc = across(lhs_ref[g], rhs)
-            cs[2 * y, 16 * g : 16 * g + 16] = acc[:, 0:TILE]
-            cs[2 * y + 1, 16 * g : 16 * g + 16] = acc[:, TILE:]
-        send_coefficients(2 * y + 1 - la % 2)
-
-        @pl.when(t != 2)
+        @pl.when(t != 3)
         def _():
-            send_coefficients(2 * y + la % 2)
+            pltpu.make_async_remote_copy(
+                src_ref=cs.at[y], dst_ref=cr.at[y_own], send_sem=many_send.at[3],
+                recv_sem=many_recv.at[3], device_id=at(2 * y + near, lo), device_id_type=MESH,
+            ).start()
 
         return carry
 
     lax.fori_loop(0, 4, analysis, 0)
-    cr[pl.ds(la, 1)] = cs[pl.ds(la, 1)]
-    love = love_ref[pl.ds(la, 1)]
-    take(many_recv, 3, cr, LATS - 1)
+    cr[pl.ds(y_own, 1)] = cs[pl.ds(y_own, 1)]
+    love = jnp.concatenate([love_ref[pl.ds(2 * y_own, 1)], love_ref[pl.ds(2 * y_own + 1, 1)]], axis=1)
+    take(many_recv, 3, cr, 3)
     coefficients = jnp.sum(cr[...], axis=0)
-    sg[pl.ds(la, 1)] = (coefficients * love).astype(bf16)[None]
-
-    def send_scaled(j, carry):
-        peer = (la + LATS - j) % LATS
+    take(many_recv, 9, db, 4)
+    coefficients = coefficients + jnp.sum(db[...].astype(f32), axis=0)
+    sg[pl.ds(y_own, 1)] = (coefficients * love).astype(bf16)[None]
+
+    def send_scaled(t, carry):
         pltpu.make_async_remote_copy(
-            src_ref=sg.at[la], dst_ref=sg.at[la], send_sem=many_send.at[4],
-            recv_sem=scaled_recv.at[la], device_id=at(peer, lo), device_id_type=MESH,
+            src_ref=sg.at[y_own], dst_ref=sg.at[y_own], send_sem=many_send.at[4],
+            recv_sem=scaled_recv.at[y_own], device_id=at(2 * y_at(t) + near, lo), device_id_type=MESH,
         ).start()
         return carry
 
-    lax.fori_loop(1, LATS, send_scaled, 0)
+    lax.fori_loop(0, 3, send_scaled, 0)
     for load in loads[15:]:
         load.wait()
 
@@ -440,21 +440,19 @@
         pltpu.make_async_copy(part, part, scaled_recv.at[owner]).wait()
 
     def synthesis(t, carry):
-        y = (la // 2 + t) % 4
+        owner = y_at(3 - t)
 
         @pl.when(t != 0)
         def _():
-            take_scaled(2 * y + la % 2)
-
-        take_scaled(2 * y + 1 - la % 2)
-        start = pl.multiple_of(y * 256, 256)
-        left = sg[2 * y]
-        right = sg[2 * y + 1]
+            take_scaled(owner)
+
+        start = pl.multiple_of(owner * QUARTER, QUARTER)
+        scaled = sg[owner]
         for g in range(4):
-            lhs = jnp.concatenate([left[16 * g : 16 * g + 16], right[16 * g : 16 * g + 16]], axis=1)
+            lhs = scaled[16 * g : 16 * g + 16]
             for k in range(4):
                 rhs = jnp.concatenate(
-                    [leg[8 * g + 2 * k + i, pl.ds(start, 256), :] for i in range(2)], axis=1
+                    [leg[8 * g + 2 * k + i, pl.ds(start, QUARTER), :] for i in range(2)], axis=1
                 )
                 acc_ref[4 * g + k] += jnp.dot(lhs, rhs, preferred_element_type=f32)
         return carry
@@ -508,26 +506,28 @@
     exchange(6, a4s, a4r)
     take(many_recv, 6, a4r, LONS - 1)
     s_out[...] = rows_of(a4r).T
-    stores[3].start()
 
     for move in halo:
         move.wait_send()
     take(many_send, 0, sum_recv, LATS - 1)
     take(many_send, 1, a1s, LONS - 1)
     take(many_send, 2, a2s, LONS - 1)
-    take(many_send, 3, cs, LATS - 1)
-    take(many_send, 4, sg, LATS - 1)
+    take(many_send, 3, cs, 3)
+    take(many_send, 9, cb, 4)
+    take(many_send, 4, sg, 3)
     take(many_send, 5, a3s, LONS - 1)
     take(many_send, 6, a4s, LONS - 1)
     take(many_send, 7, a0s, LONS - 1)
     take(many_send, 8, aws, LONS - 1)
-    for store in stores:
-        store.wait()
 
 
 def deliver(*refs):
-    for i in range(4):
-        refs[i + 4][...] = refs[i][...]
+    sems = refs[-1]
+    copies = [pltpu.make_async_copy(refs[i], refs[i + 4], sems.at[i]) for i in range(4)]
+    for copy in copies:
+        copy.start()
+    for copy in copies:
+        copy.wait()
 
 
 def shards(
@@ -543,7 +543,8 @@
     edge = pltpu.VMEM((48, TILE), f32)
     quad = pltpu.VMEM((LONS, SLOTS, TILE), f32)
     two = pltpu.VMEM((LONS, 2, TILE), f32)
-    part = pltpu.VMEM((LATS, 64, TILE), f32)
+    part = pltpu.VMEM((4, 64, QUARTER), f32)
+    rough = pltpu.VMEM((4, 64, QUARTER), bf16)
     scratch = [tile, tile, tile, tile, pltpu.VMEM((TILE, TILE), jnp.int32), tile]
     scratch += [pltpu.SMEM((8,), f32), pltpu.SMEM((8,), f32)]
     scratch += [pltpu.VMEM((LATS, LONS), jnp.int32), pltpu.VMEM((LATS, TILE), f32)]
@@ -553,35 +554,40 @@
     scratch += [pltpu.VMEM((2, 8, TILE), f32), pltpu.VMEM((2, 2, 8, TILE), f32), tile]
     scratch += [pltpu.VMEM((1, TILE), f32), pltpu.VMEM((LATS, 1, TILE), f32)]
     scratch += [quad] * 8
-    scratch += [pltpu.VMEM((4, 16, 8 * TILE), bf16), part, part, pltpu.VMEM((LATS, 64, TILE), bf16)]
+    scratch += [pltpu.VMEM((4, 16, 8 * TILE), bf16), part, part, rough, rough, rough]
     scratch += [pltpu.VMEM((16, 16, 2 * TILE), f32), two, two, quad, quad]
-    scratch += [tile] * 4
     scratch += [
         pltpu.SemaphoreType.DMA((19,)),
         pltpu.SemaphoreType.DMA((8,)), pltpu.SemaphoreType.DMA((8,)),
-        pltpu.SemaphoreType.DMA((9,)), pltpu.SemaphoreType.DMA((9,)), pltpu.SemaphoreType.DMA((8,)),
-        pltpu.SemaphoreType.DMA((4,)),
+        pltpu.SemaphoreType.DMA((10,)), pltpu.SemaphoreType.DMA((10,)), pltpu.SemaphoreType.DMA((4,)),
     ]
     results = pl.pallas_call(
         kernel,
         out_shape=(shape,) * 4,
         in_specs=[hbm] * 19,
-        out_specs=(hbm,) * 4,
+        out_specs=(vmem,) * 4,
         scratch_shapes=scratch,
         compiler_params=pltpu.CompilerParams(
             collective_id=0, has_side_effects=True, vmem_limit_bytes=VMEM_BYTES
         ),
         name="tide",
     )(
-        sea_level, east_velocity, north_velocity, depth, land_mask, loading_prev, tide_amp, tide_phase,
-        wet_counts, love_factor.reshape(LATS, NDEG // LATS), legendre,
-        *[jnp.asarray(x) for x in tables],
+        *[
+            pltpu.with_memory_space_constraint(x, pltpu.HBM)
+            for x in (
+                sea_level, east_velocity, north_velocity, depth, land_mask, loading_prev, tide_amp,
+                tide_phase, wet_counts, love_factor.reshape(LATS, NDEG // LATS), legendre,
+                *[jnp.asarray(x) for x in tables],
+            )
+        ]
     )
     return pl.pallas_call(
         deliver,
         out_shape=(shape,) * 4,
-        in_specs=[vmem] * 4,
-        out_specs=(vmem,) * 4,
+        in_specs=[pl.BlockSpec(memory_space=pl.ANY)] * 4,
+        out_specs=(hbm,) * 4,
+        scratch_shapes=[pltpu.SemaphoreType.DMA((4,))],
+        compiler_params=pltpu.CompilerParams(vmem_limit_bytes=1024 * 1024),
         name="deliver",
     )(*results)
 

time: 64.5 us -> 59.3 us (0.919)
  Pallas kernels: 63.7 us -> 58.5 us
    pallas_call x1, Pallas kernels: 62 us -> 57.8 us  [shards(): pl.pallas_call(kernel, out_shape=(shape,) * 4, in_specs=[hbm] * 19, out_s...]
    pallas_call x1, Pallas kernels: 1.64 us -> 0.73 us  [shards(): pl.pallas_call(deliver, out_shape=(shape,) * 4, in_specs=[pl.BlockSpec(me...]
where the time goes in v3:
time: 59.3 us; the launch traced here: 59.1 us
  Pallas kernels  58.5 us (99%)
  between operations  0.64 us (1%)
    pallas_call x1, Pallas kernels, shards(): pl.pallas_call(kernel, out_shape=(shape,) * 4, in_specs=[hbm] * 19, out_s...  57.8 us

profile of v3, /device:TPU:1, one launch (start us, length us, event | category | flops | bytes accessed | tf_op | source)
XLA Modules:
  0.0 59.1 jit_solution(12842405567708882828)
XLA Ops:
  0.6 57.8 %tide.1 = (f32[128,128]{1,0:T(8,128)S(1)}, f32[128,128]{1,0:T(8,128)S(1)}, f32[128,128]{1,0:T(8,128)S(1)}, f32[128,128]{1,0:T(8,128)S(1)}) custom-call(f32[128,128]{1,0:T(8,128)} %sea_hbm.1, f32[128,128]{1,0:T(8,128)} %east_hbm.1, f32[128,128]{1,0:T(8,128)} %north_hbm.1, f32[128,128]{1,0:T(8,128)} %depth_hbm.1, s32[128,128]{1,0:T(8,128)} %mask_hbm.1, ...), custom_call_target="tpu_custom_call" | custom-call | tf_op jit(solution)/shard_map/tide/pallas_call | solution.py:564
  58.4 0.7 %deliver.1 = (f32[128,128]{1,0:T(8,128)}, f32[128,128]{1,0:T(8,128)}, f32[128,128]{1,0:T(8,128)}, f32[128,128]{1,0:T(8,128)}) custom-call(f32[128,128]{1,0:T(8,128)S(1)} %get-tuple-element.8.refs_0_, f32[128,128]{1,0:T(8,128)S(1)} %get-tuple-element.9.refs_1_, f32[128,128]{1,0:T(8,128)S(1)} %get-tuple-element.10.refs_2_, ...), custom_call_target="tpu_custom_call" | custom-call | tf_op jit(solution)/shard_map/deliver/pallas_call | solution.py:584

commit v4 on v3

--- a/solution.py
+++ b/solution.py
@@ -75,15 +75,16 @@
         for row in range(ROWS):
             for r in range(2):
                 place[s, r, row, r, ROWS * s + row] = 1.0
-    spread = place[:, :2].reshape(64, 1024)
+    spread = place[:, :2].reshape(8, 4, 2, 1024).transpose(0, 2, 1, 3).reshape(64, 1024)
     place = place.reshape(128, 1024)
     cos, sin = turn(np.outer(cell, band), 128)
-    back = np.zeros((2, 128, 32, 2))
-    back[0, :, :, 0] = cos
-    back[0, :, :, 1] = -sin
-    back[1, :, :, 0] = sin
-    back[1, :, :, 1] = cos
-    back = back.reshape(256, 64)
+    back = np.zeros((4, 2, 128, 32, 2, 4))
+    for quad in range(4):
+        back[quad, 0, :, :, 0, quad] = cos
+        back[quad, 0, :, :, 1, quad] = -sin
+        back[quad, 1, :, :, 0, quad] = sin
+        back[quad, 1, :, :, 1, quad] = cos
+    back = back.reshape(1024, 256)
     cos, sin = turn(np.outer(cell, band), 4096)
     untwist = np.stack([np.tile(cos, (1, ROWS)), np.tile(sin, (1, ROWS))])
     cos, sin = turn(np.outer(band, band), 32)
@@ -94,7 +95,7 @@
     last = last.reshape(128, 256)
     plain = [x.astype(np.float32) for x in (twist, untwist)]
     exact = [x.astype(ml_dtypes.bfloat16) for x in (place, spread)]
-    return [split(first), plain[0], split(second), exact[0], split(back), plain[1], split(last), exact[1]]
+    return [split(first), plain[0], split(second), exact[0], split(back)[:, 256:], plain[1], split(last), exact[1]]
 
 
 def halves(value, axis):
@@ -282,9 +283,10 @@
     def rows_of(buffer):
         return jnp.concatenate([buffer[s] for s in range(LONS)], axis=0)
 
+    for move in halo[6:]:
+        move.wait_recv()
     exchange(7, a0s, a0r)
-
-    for move in halo:
+    for move in halo[0:6]:
         move.wait_recv()
 
     has_lo = jnp.where(la > 0, 1.0, 0.0).astype(f32)
@@ -486,26 +488,50 @@
         ],
         axis=0,
     )
-    large = stacked.astype(bf16)
-    tiny = (stacked - large.astype(f32)).astype(bf16)
-    rows = across(spread[...], large) + across(spread[...], tiny)
-    for s in range(LONS):
-        a3s[s] = rows[2 * s : 2 * s + 2]
-    exchange(5, a3s, a3r)
+    rows = across(spread[...], stacked.astype(bf16))
+    a3s[...] = rows.astype(bf16).reshape(8, 8, TILE)
+
+    def send_rows(peer):
+        pltpu.make_async_remote_copy(
+            src_ref=a3s.at[peer % 8], dst_ref=a3r.at[lo], send_sem=many_send.at[5],
+            recv_sem=many_recv.at[5], device_id=at(la, peer), device_id_type=MESH,
+        ).start()
+
+    for dx in (2, 1, 3, 0):
+
+        def send_block(j, carry, dx=dx):
+            send_rows((lo // 8 + dx) % 4 * 8 + (lo + j) % 8)
+            return carry
+
+        lax.fori_loop(1 if dx == 0 else 0, 8, send_block, 0)
+    a3r[pl.ds(lo, 1)] = a3s[pl.ds(lo % 8, 1)]
     take(many_recv, 5, a3r, LONS - 1)
 
-    opened = jnp.dot(back[...], halves(rows_of(a3r), 0), preferred_element_type=f32)
-    re = opened[0:TILE]
-    im = opened[TILE:]
+    every = a3r[...].reshape(256, TILE)
+    opened = jnp.dot(back[...], jnp.concatenate([every, every], axis=0), preferred_element_type=f32)
     cos_u = untwist[0]
     sin_u = untwist[1]
-    untwisted = jnp.concatenate([re * cos_u - im * sin_u, re * sin_u + im * cos_u], axis=1)
-    field = across(last[...], halves(untwisted, 1))
-    for s in range(LONS):
-        a4s[s] = field[ROWS * s : ROWS * s + ROWS]
-    exchange(6, a4s, a4r)
-    take(many_recv, 6, a4r, LONS - 1)
-    s_out[...] = rows_of(a4r).T
+    mine = last[pl.ds(pl.multiple_of(lo // 8 * 32, 32), 32), :]
+    for quad in range(4):
+        re = opened[256 * quad : 256 * quad + TILE]
+        im = opened[256 * quad + TILE : 256 * quad + 256]
+        untwisted = jnp.concatenate([re * cos_u - im * sin_u, re * sin_u + im * cos_u], axis=1)
+        field = across(mine, halves(untwisted, 1))
+        for e in range(8):
+            a4s[e, 4 * quad : 4 * quad + 4] = field[4 * e : 4 * e + 4]
+
+    def send_field(j, carry):
+        e = (lo + j) % 8
+        pltpu.make_async_remote_copy(
+            src_ref=a4s.at[e], dst_ref=a4r.at[lo % 8], send_sem=many_send.at[6],
+            recv_sem=many_recv.at[6], device_id=at(la, lo // 8 * 8 + e), device_id_type=MESH,
+        ).start()
+        return carry
+
+    lax.fori_loop(1, 8, send_field, 0)
+    a4r[pl.ds(lo % 8, 1)] = a4s[pl.ds(lo % 8, 1)]
+    take(many_recv, 6, a4r, 7)
+    s_out[...] = a4r[...].reshape(TILE, TILE).T
 
     for move in halo:
         move.wait_send()
@@ -515,8 +541,8 @@
     take(many_send, 3, cs, 3)
     take(many_send, 9, cb, 4)
     take(many_send, 4, sg, 3)
-    take(many_send, 5, a3s, LONS - 1)
-    take(many_send, 6, a4s, LONS - 1)
+    take(many_send, 5, a3r, LONS - 1)
+    take(many_send, 6, a4s, 7)
     take(many_send, 7, a0s, LONS - 1)
     take(many_send, 8, aws, LONS - 1)
 
@@ -542,7 +568,6 @@
     slab = pltpu.VMEM((FIELDS, 8, TILE), f32)
     edge = pltpu.VMEM((48, TILE), f32)
     quad = pltpu.VMEM((LONS, SLOTS, TILE), f32)
-    two = pltpu.VMEM((LONS, 2, TILE), f32)
     part = pltpu.VMEM((4, 64, QUARTER), f32)
     rough = pltpu.VMEM((4, 64, QUARTER), bf16)
     scratch = [tile, tile, tile, tile, pltpu.VMEM((TILE, TILE), jnp.int32), tile]
@@ -555,7 +580,8 @@
     scratch += [pltpu.VMEM((1, TILE), f32), pltpu.VMEM((LATS, 1, TILE), f32)]
     scratch += [quad] * 8
     scratch += [pltpu.VMEM((4, 16, 8 * TILE), bf16), part, part, rough, rough, rough]
-    scratch += [pltpu.VMEM((16, 16, 2 * TILE), f32), two, two, quad, quad]
+    scratch += [pltpu.VMEM((16, 16, 2 * TILE), f32), pltpu.VMEM((8, 8, TILE), bf16)]
+    scratch += [pltpu.VMEM((LONS, 8, TILE), bf16)] + [pltpu.VMEM((8, 16, TILE), f32)] * 2
     scratch += [
         pltpu.SemaphoreType.DMA((19,)),
         pltpu.SemaphoreType.DMA((8,)), pltpu.SemaphoreType.DMA((8,)),

time: 59.3 us -> 58.4 us (0.985)
  Pallas kernels: 58.5 us -> 57.6 us
    pallas_call x1, Pallas kernels: 57.8 us -> 56.9 us  [shards(): pl.pallas_call(kernel, out_shape=(shape,) * 4, in_specs=[hbm] * 19, out_s...]
where the time goes in v4:
time: 58.4 us; the launch traced here: 58.3 us
  Pallas kernels  57.6 us (99%)
  between operations  0.64 us (1%)
    pallas_call x1, Pallas kernels, shards(): pl.pallas_call(kernel, out_shape=(shape,) * 4, in_specs=[hbm] * 19, out_s...  56.9 us

profile of v4, /device:TPU:1, one launch (start us, length us, event | category | flops | bytes accessed | tf_op | source)
XLA Modules:
  0.0 58.3 jit_solution(10972674325781684161)
XLA Ops:
  0.6 56.9 %tide.1 = (f32[128,128]{1,0:T(8,128)S(1)}, f32[128,128]{1,0:T(8,128)S(1)}, f32[128,128]{1,0:T(8,128)S(1)}, f32[128,128]{1,0:T(8,128)S(1)}) custom-call(f32[128,128]{1,0:T(8,128)} %sea_hbm.1, f32[128,128]{1,0:T(8,128)} %east_hbm.1, f32[128,128]{1,0:T(8,128)} %north_hbm.1, f32[128,128]{1,0:T(8,128)} %depth_hbm.1, s32[128,128]{1,0:T(8,128)} %mask_hbm.1, ...), custom_call_target="tpu_custom_call" | custom-call | tf_op jit(solution)/shard_map/tide/pallas_call | solution.py:590
  57.6 0.7 %deliver.1 = (f32[128,128]{1,0:T(8,128)}, f32[128,128]{1,0:T(8,128)}, f32[128,128]{1,0:T(8,128)}, f32[128,128]{1,0:T(8,128)}) custom-call(f32[128,128]{1,0:T(8,128)S(1)} %get-tuple-element.8.refs_0_, f32[128,128]{1,0:T(8,128)S(1)} %get-tuple-element.9.refs_1_, f32[128,128]{1,0:T(8,128)S(1)} %get-tuple-element.10.refs_2_, ...), custom_call_target="tpu_custom_call" | custom-call | tf_op jit(solution)/shard_map/deliver/pallas_call | solution.py:610

commit v5 on v4

--- a/solution.py
+++ b/solution.py
@@ -164,9 +164,6 @@
     loads = [
         pltpu.make_async_copy(src, dst, local_sem.at[i]) for i, (src, dst) in enumerate(pairs)
     ]
-    for load in loads[0:6]:
-        load.start()
-
     barrier = pltpu.get_barrier_semaphore()
 
     def greet_lon(j, carry):
@@ -181,6 +178,8 @@
     for dl in (1, LATS - 1):
         for dn in (1, LONS - 1):
             pl.semaphore_signal(barrier, inc=1, device_id=at(la + dl, lo + dn), device_id_type=MESH)
+    for load in loads[0:6]:
+        load.start()
     lax.fori_loop(1, LONS, greet_lon, 0)
     for load in loads[6:]:
         load.start()
@@ -354,14 +353,15 @@
     for s in range(LONS):
         aws[s] = full[SLOTS * s : SLOTS * s + SLOTS]
     exchange(8, aws, awr)
+    take(many_recv, 1, a1r, LONS - 1)
+    full = analyse(jnp.dot(first[...], halves(rows_of(a1r), 0), preferred_element_type=f32))
+    for s in range(LONS):
+        a2s[s] = full[SLOTS * s : SLOTS * s + SLOTS]
     take(many_recv, 0, sum_recv, LATS - 1)
     band_sum = jnp.sum(sum_recv[...], axis=0)
-    take(many_recv, 1, a1r, LONS - 1)
-    full = analyse(jnp.dot(first[...], halves(rows_of(a1r), 0), preferred_element_type=f32))
     kind_row = lax.broadcasted_iota(jnp.int32, (TILE, TILE), 0) % SLOTS
-    full = jnp.where(kind_row == 2, band_sum, full)
     for s in range(LONS):
-        a2s[s] = full[SLOTS * s : SLOTS * s + SLOTS]
+        a2s[s, 2:3] = band_sum
     exchange(2, a2s, a2r)
     for load in loads[12:15]:
         load.wait()

time: 58.4 us -> 58.2 us (level)
  no operation moved by 1% of the time
where the time goes in v5:
time: 58.2 us; the launch traced here: 58.1 us
  Pallas kernels  57.5 us (99%)
  between operations  0.64 us (1%)
    pallas_call x1, Pallas kernels, shards(): pl.pallas_call(kernel, out_shape=(shape,) * 4, in_specs=[hbm] * 19, out_s...  56.7 us

profile of v5, /device:TPU:1, one launch (start us, length us, event | category | flops | bytes accessed | tf_op | source)
XLA Modules:
  0.0 58.1 jit_solution(10450541140311866579)
XLA Ops:
  0.6 56.7 %tide.1 = (f32[128,128]{1,0:T(8,128)S(1)}, f32[128,128]{1,0:T(8,128)S(1)}, f32[128,128]{1,0:T(8,128)S(1)}, f32[128,128]{1,0:T(8,128)S(1)}) custom-call(f32[128,128]{1,0:T(8,128)} %sea_hbm.1, f32[128,128]{1,0:T(8,128)} %east_hbm.1, f32[128,128]{1,0:T(8,128)} %north_hbm.1, f32[128,128]{1,0:T(8,128)} %depth_hbm.1, s32[128,128]{1,0:T(8,128)} %mask_hbm.1, ...), custom_call_target="tpu_custom_call" | custom-call | tf_op jit(solution)/shard_map/tide/pallas_call | solution.py:590
  57.4 0.7 %deliver.1 = (f32[128,128]{1,0:T(8,128)}, f32[128,128]{1,0:T(8,128)}, f32[128,128]{1,0:T(8,128)}, f32[128,128]{1,0:T(8,128)}) custom-call(f32[128,128]{1,0:T(8,128)S(1)} %get-tuple-element.8.refs_0_, f32[128,128]{1,0:T(8,128)S(1)} %get-tuple-element.9.refs_1_, f32[128,128]{1,0:T(8,128)S(1)} %get-tuple-element.10.refs_2_, ...), custom_call_target="tpu_custom_call" | custom-call | tf_op jit(solution)/shard_map/deliver/pallas_call | solution.py:610

commit v6 on v5

--- a/solution.py
+++ b/solution.py
@@ -158,7 +158,7 @@
         (sea_hbm, sea_ref), (east_hbm, east_ref), (north_hbm, north_ref), (depth_hbm, depth_ref),
         (mask_hbm, mask_ref), (load_hbm, load_ref), (amp_hbm, amp_ref), (phase_hbm, phase_ref),
         (twist_hbm, twist), (first_hbm, first), (second_hbm, second), (place_hbm, place),
-        (counts_hbm, counts_ref), (leg_hbm, leg), (love_hbm, love_ref), (spread_hbm, spread),
+        (counts_hbm, counts_ref), (leg_hbm, leg), (love_hbm, love_ref.at[pl.ds(0, LATS)]), (spread_hbm, spread),
         (back_hbm, back), (untwist_hbm, untwist), (last_hbm, last),
     )
     loads = [
@@ -310,12 +310,13 @@
     h = h[MARGIN : MARGIN + TILE, 0:TILE]
     wet_h = wet_core * h
 
-    sum_send[...] = jnp.sum(wet_h, axis=0, keepdims=True)
-    sum_recv[pl.ds(la, 1)] = sum_send[...][None]
+    own_sum = jnp.sum(wet_h, axis=0, keepdims=True)
+    sum_send[0] = own_sum
+    sum_recv[pl.ds(la, 1)] = own_sum[None]
 
     def send_sum(j, carry):
         pltpu.make_async_remote_copy(
-            src_ref=sum_send, dst_ref=sum_recv.at[la], send_sem=many_send.at[0],
+            src_ref=sum_send.at[0], dst_ref=sum_recv.at[la], send_sem=many_send.at[0],
             recv_sem=many_recv.at[0], device_id=at(la + j, lo), device_id_type=MESH,
         ).start()
         return carry
@@ -358,7 +359,7 @@
     for s in range(LONS):
         a2s[s] = full[SLOTS * s : SLOTS * s + SLOTS]
     take(many_recv, 0, sum_recv, LATS - 1)
-    band_sum = jnp.sum(sum_recv[...], axis=0)
+    band_sum = jnp.sum(sum_recv[0:LATS], axis=0)
     kind_row = lax.broadcasted_iota(jnp.int32, (TILE, TILE), 0) % SLOTS
     for s in range(LONS):
         a2s[s, 2:3] = band_sum
@@ -489,7 +490,7 @@
         axis=0,
     )
     rows = across(spread[...], stacked.astype(bf16))
-    a3s[...] = rows.astype(bf16).reshape(8, 8, TILE)
+    a3s[0:8] = rows.astype(bf16).reshape(8, 8, TILE)
 
     def send_rows(peer):
         pltpu.make_async_remote_copy(
@@ -507,7 +508,7 @@
     a3r[pl.ds(lo, 1)] = a3s[pl.ds(lo % 8, 1)]
     take(many_recv, 5, a3r, LONS - 1)
 
-    every = a3r[...].reshape(256, TILE)
+    every = a3r[0:LONS].reshape(256, TILE)
     opened = jnp.dot(back[...], jnp.concatenate([every, every], axis=0), preferred_element_type=f32)
     cos_u = untwist[0]
     sin_u = untwist[1]
@@ -567,21 +568,21 @@
     tile = pltpu.VMEM((TILE, TILE), f32)
     slab = pltpu.VMEM((FIELDS, 8, TILE), f32)
     edge = pltpu.VMEM((48, TILE), f32)
-    quad = pltpu.VMEM((LONS, SLOTS, TILE), f32)
+    quad = pltpu.VMEM((LONS + 2, SLOTS, TILE), f32)
     part = pltpu.VMEM((4, 64, QUARTER), f32)
     rough = pltpu.VMEM((4, 64, QUARTER), bf16)
     scratch = [tile, tile, tile, tile, pltpu.VMEM((TILE, TILE), jnp.int32), tile]
     scratch += [pltpu.SMEM((8,), f32), pltpu.SMEM((8,), f32)]
-    scratch += [pltpu.VMEM((LATS, LONS), jnp.int32), pltpu.VMEM((LATS, TILE), f32)]
+    scratch += [pltpu.VMEM((LATS, LONS), jnp.int32), pltpu.VMEM((2 * LATS, TILE), f32)]
     scratch += [pltpu.VMEM((WAVES, NDEG, TILE), bf16)]
     scratch += [pltpu.VMEM(x.shape, x.dtype) for x in tables]
     scratch += [edge, edge, edge, edge, slab, slab, slab, slab]
     scratch += [pltpu.VMEM((2, 8, TILE), f32), pltpu.VMEM((2, 2, 8, TILE), f32), tile]
-    scratch += [pltpu.VMEM((1, TILE), f32), pltpu.VMEM((LATS, 1, TILE), f32)]
+    scratch += [pltpu.VMEM((LATS, 1, TILE), f32), pltpu.VMEM((2 * LATS, 1, TILE), f32)]
     scratch += [quad] * 8
     scratch += [pltpu.VMEM((4, 16, 8 * TILE), bf16), part, part, rough, rough, rough]
-    scratch += [pltpu.VMEM((16, 16, 2 * TILE), f32), pltpu.VMEM((8, 8, TILE), bf16)]
-    scratch += [pltpu.VMEM((LONS, 8, TILE), bf16)] + [pltpu.VMEM((8, 16, TILE), f32)] * 2
+    scratch += [pltpu.VMEM((16, 16, 2 * TILE), f32), pltpu.VMEM((10, 8, TILE), bf16)]
+    scratch += [pltpu.VMEM((LONS + 2, 8, TILE), bf16)] + [pltpu.VMEM((8, 16, TILE), f32)] * 2
     scratch += [
         pltpu.SemaphoreType.DMA((19,)),
         pltpu.SemaphoreType.DMA((8,)), pltpu.SemaphoreType.DMA((8,)),

time: 58.2 us -> 58.2 us (level)
  no operation moved by 1% of the time
where the time goes in v6:
time: 58.2 us; the launch traced here: 58.1 us
  Pallas kernels  57.5 us (99%)
  between operations  0.64 us (1%)
    pallas_call x1, Pallas kernels, shards(): pl.pallas_call(kernel, out_shape=(shape,) * 4, in_specs=[hbm] * 19, out_s...  56.7 us

profile of v6, /device:TPU:1, one launch (start us, length us, event | category | flops | bytes accessed | tf_op | source)
XLA Modules:
  0.0 58.1 jit_solution(14613508632343025428)
XLA Ops:
  0.6 56.7 %tide.1 = (f32[128,128]{1,0:T(8,128)S(1)}, f32[128,128]{1,0:T(8,128)S(1)}, f32[128,128]{1,0:T(8,128)S(1)}, f32[128,128]{1,0:T(8,128)S(1)}) custom-call(f32[128,128]{1,0:T(8,128)} %sea_hbm.1, f32[128,128]{1,0:T(8,128)} %east_hbm.1, f32[128,128]{1,0:T(8,128)} %north_hbm.1, f32[128,128]{1,0:T(8,128)} %depth_hbm.1, s32[128,128]{1,0:T(8,128)} %mask_hbm.1, ...), custom_call_target="tpu_custom_call" | custom-call | tf_op jit(solution)/shard_map/tide/pallas_call | solution.py:591
  57.4 0.7 %deliver.1 = (f32[128,128]{1,0:T(8,128)}, f32[128,128]{1,0:T(8,128)}, f32[128,128]{1,0:T(8,128)}, f32[128,128]{1,0:T(8,128)}) custom-call(f32[128,128]{1,0:T(8,128)S(1)} %get-tuple-element.8.refs_0_, f32[128,128]{1,0:T(8,128)S(1)} %get-tuple-element.9.refs_1_, f32[128,128]{1,0:T(8,128)S(1)} %get-tuple-element.10.refs_2_, ...), custom_call_target="tpu_custom_call" | custom-call | tf_op jit(solution)/shard_map/deliver/pallas_call | solution.py:611
